TPU v7x, 32 devices: a whole 2x2x4 slice. The times are simulated.
32 devices in a mesh: shard: 4 (over y, x), dp: 8 (over z, core).
Axes of the slice: x: 2, y: 2, z: 4, core: 2. Of those that a mesh axis runs over, the one named last changes fastest.
Arguments:
- inputs: bfloat16 [8, 512, 1088], P('dp', 'shard')
- segment: int32 [8, 512], P('dp'), may hold values from 0 to 3, never falling along the last dimension, each value on 1 to 256 neighbouring positions
- cotangent: bfloat16 [8, 512, 1088], P('dp', 'shard'), may hold values from -6 to 6
- query_weight: bfloat16 [1088, 1088], P('shard')
- key_weight: bfloat16 [1088, 1088], P('shard')
- value_weight: bfloat16 [1088, 1088], P('shard'), may hold values from -0.1875 to 0.1875
- out_weight: bfloat16 [1088, 1088], P('shard'), may hold values from -3 to 3
- up_weight: bfloat16 [1088, 4352], P('shard'), may hold values from -0.1875 to 0.1875
- down_weight: bfloat16 [4352, 1088], P('shard'), may hold values from -0.09375 to 0.09375
- query_bias: bfloat16 [1088], P('shard'), may hold values from -3 to 3
- value_bias: bfloat16 [1088], P('shard'), may hold values from -3 to 3
- out_bias: bfloat16 [1088], P('shard'), may hold values from -3 to 3
- up_bias: bfloat16 [4352], P('shard'), may hold values from -3 to 3
- down_bias: bfloat16 [1088], P('shard'), may hold values from -3 to 3
- first_gain: bfloat16 [1088], P('shard'), may hold values from 0.5 to 1.5
- first_shift: bfloat16 [1088], P('shard'), may hold values from -3 to 3
- second_gain: bfloat16 [1088], P('shard'), may hold values from 0.5 to 1.5
- second_shift: bfloat16 [1088], P('shard'), may hold values from -3 to 3
Outputs:
- outputs: bfloat16 [8, 512, 1088], P('dp', 'shard')
- input_grad: float32 [8, 512, 1088], P('dp', 'shard')
- query_weight_grad: float32 [1088, 1088], P('shard')
- key_weight_grad: float32 [1088, 1088], P('shard')
- value_weight_grad: float32 [1088, 1088], P('shard')
- out_weight_grad: float32 [1088, 1088], P('shard')
- up_weight_grad: float32 [1088, 4352], P('shard')
- down_weight_grad: float32 [4352, 1088], P('shard')
- query_bias_grad: float32 [1088], P('shard')
- value_bias_grad: float32 [1088], P('shard')
- out_bias_grad: float32 [1088], P('shard')
- up_bias_grad: float32 [4352], P('shard')
- down_bias_grad: float32 [1088], P('shard')
- first_gain_grad: float32 [1088], P('shard')
- first_shift_grad: float32 [1088], P('shard')
- second_gain_grad: float32 [1088], P('shard')
- second_shift_grad: float32 [1088], P('shard')
Inputs may be any that keep to these rules, and one draw needn't show every extreme that they name: `segment`: along each sequence the document numbers never fall; each of the 4 documents holds 1 to 256 tokens and one holds exactly 256.
All inputs are finite; a program needn't handle non-finite values.
Results may differ from a plain program's by a relative error of at most 0.018.
The roundings to bfloat16 on the way count: a program that leaves them out, or rounds other values in their place, can miss the bound.
Values may be sent and summed in bfloat16 or wider, within the bound.
No kernel may reach another device: no remote copies, remote signals or barrier semaphores. Data moves between devices by JAX's collectives and lax.ppermute only.
A program may use at most 192 MiB of HBM per device.

v0:
```python
from functools import partial

import jax
import jax.numpy as jnp
from jax import lax
from jax.experimental import pallas as pl
from jax.experimental.pallas import tpu as pltpu
from jax.sharding import PartitionSpec as P


HEADS = 17
HD = 64
EPSILON = 1e-05
SCORE_SCALE = 0.125
MASKED_SCORE = -1e30
LANES = 128
MANY = 4


BF16 = jnp.bfloat16
F32 = jnp.float32


def normalise(values):
    average = jnp.mean(values, axis=-1, keepdims=True)
    centred = values - average
    variance = jnp.mean(centred * centred, axis=-1, keepdims=True)
    inv_std = lax.rsqrt(variance + EPSILON)
    return centred * inv_std, inv_std


def norm_backward(grad_normed, normed, inv_std, gain_vec):
    scaled = grad_normed * gain_vec
    first_mean = jnp.mean(scaled, axis=-1, keepdims=True)
    second_mean = jnp.mean(scaled * normed, axis=-1, keepdims=True)
    return inv_std * (scaled - first_mean - normed * second_mean)


def matmul(left_side, right_side):
    return jnp.dot(left_side, right_side, preferred_element_type=F32)


def contract_rows(left_side, right_side):
    return lax.dot_general(
        left_side, right_side, (((0,), (0,)), ((), ())), preferred_element_type=F32
    )


def contract_last(left_side, right_side):
    return lax.dot_general(
        left_side, right_side, (((1,), (1,)), ((), ())), preferred_element_type=F32
    )


def mask_bias(row_seg, row_pos, col_seg, col_pos):
    allowed = (row_seg == col_seg) & (col_pos <= row_pos)
    return jnp.where(allowed, 0.0, MASKED_SCORE)


def attention_forward(qkv, rows_info, cols_info, heads):
    tokens = qkv.shape[0]
    width = heads * HD
    block = min(256, tokens)

    def kernel(q_ref, kv_ref, rows_ref, cols_ref, out_ref, log_ref):
        bias = mask_bias(
            rows_ref[:, 0:1], rows_ref[:, 1:2], cols_ref[0:1, :], cols_ref[1:2, :]
        )
        lane = lax.broadcasted_iota(jnp.int32, (block, LANES), 1)
        logs = jnp.zeros((block, LANES), F32)
        for h in range(heads):
            query = q_ref[:, h * HD : (h + 1) * HD]
            keys = kv_ref[:, width + h * HD : width + (h + 1) * HD]
            vals = kv_ref[:, 2 * width + h * HD : 2 * width + (h + 1) * HD]
            scores = contract_last(query, keys) * SCORE_SCALE + bias
            largest = jnp.max(scores, axis=1, keepdims=True)
            grown = jnp.exp(scores - largest)
            total = jnp.sum(grown, axis=1, keepdims=True)
            probs = (grown * (1.0 / total)).astype(BF16)
            out_ref[:, h * HD : (h + 1) * HD] = matmul(probs, vals).astype(BF16)
            logs = jnp.where(lane == h, largest + jnp.log(total), logs)
        log_ref[...] = logs

    return pl.pallas_call(
        kernel,
        grid=(tokens // block,),
        in_specs=[
            pl.BlockSpec((block, 3 * width), lambda b: (b, 0)),
            pl.BlockSpec((tokens, 3 * width), lambda b: (0, 0)),
            pl.BlockSpec((block, 2), lambda b: (b, 0)),
            pl.BlockSpec((2, tokens), lambda b: (0, 0)),
        ],
        out_specs=[
            pl.BlockSpec((block, width), lambda b: (b, 0)),
            pl.BlockSpec((block, LANES), lambda b: (b, 0)),
        ],
        out_shape=[
            jax.ShapeDtypeStruct((tokens, width), BF16),
            jax.ShapeDtypeStruct((tokens, LANES), F32),
        ],
        name="attention_forward",
    )(qkv, qkv, rows_info, cols_info)


def attention_backward(qkv, grad_att, attended, logs, rows_info, cols_info, heads):
    tokens = qkv.shape[0]
    width = heads * HD
    block = min(256, tokens)
    steps = tokens // block

    def kernel(
        q_ref, kv_ref, grad_ref, att_ref, log_ref, rows_ref, cols_ref,
        gq_ref, gkv_ref, sums_ref, acc_ref, bias_ref,
    ):
        step = pl.program_id(0)

        @pl.when(step == 0)
        def _():
            acc_ref[...] = jnp.zeros_like(acc_ref)
            bias_ref[...] = jnp.zeros_like(bias_ref)

        bias = mask_bias(
            rows_ref[:, 0:1], rows_ref[:, 1:2], cols_ref[0:1, :], cols_ref[1:2, :]
        )
        for h in range(heads):
            own = slice(h * HD, (h + 1) * HD)
            query = q_ref[:, own]
            keys = kv_ref[:, width + h * HD : width + (h + 1) * HD]
            vals = kv_ref[:, 2 * width + h * HD : 2 * width + (h + 1) * HD]
            grad = grad_ref[:, own]
            delta = jnp.sum(
                grad.astype(F32) * att_ref[:, own].astype(F32), axis=1, keepdims=True
            )
            scores = contract_last(query, keys) * SCORE_SCALE + bias
            exact = jnp.exp(scores - log_ref[:, h : h + 1])
            grad_probs = contract_last(grad, vals)
            grad_scores = (exact * (grad_probs - delta) * SCORE_SCALE).astype(BF16)
            grad_query = matmul(grad_scores, keys)
            gq_ref[:, own] = grad_query.astype(BF16)
            bias_ref[0:1, own] += jnp.sum(grad_query, axis=0, keepdims=True)
            acc_ref[:, own] += contract_rows(grad_scores, query)
            acc_ref[:, width + h * HD : width + (h + 1) * HD] += contract_rows(
                exact.astype(BF16), grad
            )

        @pl.when(step == steps - 1)
        def _():
            gkv_ref[...] = acc_ref[...].astype(BF16)
            bias_ref[1:2, :] = jnp.sum(acc_ref[:, width:], axis=0, keepdims=True)
            sums_ref[...] = bias_ref[...]

    return pl.pallas_call(
        kernel,
        grid=(steps,),
        in_specs=[
            pl.BlockSpec((block, 3 * width), lambda b: (b, 0)),
            pl.BlockSpec((tokens, 3 * width), lambda b: (0, 0)),
            pl.BlockSpec((block, width), lambda b: (b, 0)),
            pl.BlockSpec((block, width), lambda b: (b, 0)),
            pl.BlockSpec((block, LANES), lambda b: (b, 0)),
            pl.BlockSpec((block, 2), lambda b: (b, 0)),
            pl.BlockSpec((2, tokens), lambda b: (0, 0)),
        ],
        out_specs=[
            pl.BlockSpec((block, width), lambda b: (b, 0)),
            pl.BlockSpec((tokens, 2 * width), lambda b: (0, 0)),
            pl.BlockSpec((8, width), lambda b: (0, 0)),
        ],
        out_shape=[
            jax.ShapeDtypeStruct((tokens, width), BF16),
            jax.ShapeDtypeStruct((tokens, 2 * width), BF16),
            jax.ShapeDtypeStruct((8, width), F32),
        ],
        scratch_shapes=[
            pltpu.VMEM((tokens, 2 * width), F32),
            pltpu.VMEM((8, width), F32),
        ],
        name="attention_backward",
    )(qkv, qkv, grad_att, attended, logs, rows_info, cols_info)


def on_device_general(
    count,
    inputs,
    segment,
    cotangent,
    query_weight,
    key_weight,
    value_weight,
    out_weight,
    up_weight,
    down_weight,
    query_bias,
    value_bias,
    out_bias,
    up_bias,
    down_bias,
    first_gain,
    first_shift,
    second_gain,
    second_shift,
):
    me = lax.axis_index("shard")
    others = range(1, count)
    order = me ^ jnp.arange(count, dtype=jnp.int32)
    length = inputs.shape[1]
    model = inputs.shape[2]
    own = query_weight.shape[0]
    hidden = down_weight.shape[0]
    per = -(-HEADS // count)
    width = per * HD
    padded = count * width

    def send(value, k):
        return lax.ppermute(value, "shard", [(j, j ^ k) for j in range(count)])

    def gather(value):
        if count > MANY:
            whole = lax.all_gather(value, "shard")
            return [lax.dynamic_index_in_dim(whole, me ^ k, 0, False) for k in range(count)]
        return [value] + [send(value, k) for k in others]

    def swap(pieces):
        if count > MANY:
            whole = jnp.stack(pieces)[order]
            whole = lax.all_to_all(whole, "shard", split_axis=0, concat_axis=0)[order]
            return [whole[k] for k in range(count)]
        return [pieces[0]] + [send(pieces[k], k) for k in others]

    def scatter_sum(partial_rows):
        blocks = [partial_rows[k * length : (k + 1) * length] for k in range(count)]
        got = swap([b.astype(BF16) for b in blocks])
        return sum((v.astype(F32) for v in got[1:]), blocks[0])

    def in_order(pieces):
        rows = pieces[0].shape[0]
        whole = jnp.zeros((count * rows,) + pieces[0].shape[1:], pieces[0].dtype)
        for k in range(count):
            start = ((me ^ k) * rows,) + (0,) * (pieces[0].ndim - 1)
            whole = lax.dynamic_update_slice(whole, pieces[k], start)
        return whole

    def exchange(stacked):
        return swap(
            [lax.dynamic_index_in_dim(stacked, me ^ k, 0, False) for k in range(count)]
        )

    vectors = jnp.stack(
        [
            query_bias, value_bias, out_bias, down_bias,
            first_gain, first_shift, second_gain, second_shift,
        ]
    )
    vectors = in_order([v[None] for v in gather(vectors)])
    vectors = vectors.transpose(1, 0, 2).reshape(8, model).astype(F32)
    all_inputs = jnp.concatenate(gather(inputs[0]), axis=0)
    pad_cols = lambda w: jnp.pad(w, ((0, 0), (0, padded - model)))
    stacked_qkv = jnp.concatenate(
        [
            pad_cols(w).reshape(own, count, width)
            for w in (query_weight, key_weight, value_weight)
        ],
        axis=2,
    ).transpose(1, 0, 2)
    qkv_cols = in_order(exchange(stacked_qkv))
    all_cot = jnp.concatenate(gather(cotangent[0]), axis=0)
    full_out = jnp.pad(in_order(gather(out_weight)), ((0, padded - model), (0, 0)))
    head_out = lax.dynamic_slice_in_dim(full_out, me * width, width, axis=0)
    mixed_out = full_out.reshape(count, width, model)[order].reshape(padded, model)
    up_cols = in_order(exchange(up_weight.reshape(own, count, hidden).transpose(1, 0, 2)))

    pos = (order[:, None] * length + jnp.arange(length, dtype=jnp.int32)[None, :]).reshape(-1)
    seg = segment[0].reshape(count, length)[order].reshape(-1)
    rows_info = jnp.stack([seg, pos], axis=1)
    cols_info = jnp.stack([seg, pos], axis=0)

    head_slice = lambda v: lax.dynamic_slice_in_dim(
        jnp.pad(v, (0, padded - model)), me * width, width
    )
    qkv_bias = jnp.concatenate(
        [head_slice(vectors[0]), jnp.zeros((width,), F32), head_slice(vectors[1])]
    )

    first_gain_full, first_shift_full = vectors[4], vectors[5]
    second_gain_full, second_shift_full = vectors[6], vectors[7]
    all_hat, _ = normalise(all_inputs.astype(F32))
    first_in = (all_hat * first_gain_full + first_shift_full).astype(BF16)
    qkv = (matmul(first_in, qkv_cols) + qkv_bias).astype(BF16)
    attended, logs = attention_forward(qkv, rows_info, cols_info, per)
    att_pieces = swap([attended[k * length : (k + 1) * length] for k in range(count)])
    residual_in = inputs[0].astype(F32)
    own_attended = jnp.concatenate(att_pieces, axis=1)
    middle = residual_in + matmul(own_attended, mixed_out) + vectors[2]
    second_hat, second_inv = normalise(middle)
    own_second_in = (second_hat * second_gain_full + second_shift_full).astype(BF16)
    second_in = jnp.concatenate(gather(own_second_in), axis=0)
    pre_act = matmul(second_in, up_cols) + up_bias.astype(F32)
    below = 0.5 * (1.0 + lax.erf(pre_act * (0.5**0.5)))
    activated = (pre_act * below).astype(BF16)
    slope = below + pre_act * (jnp.exp(-0.5 * pre_act * pre_act) * 0.3989422804014327)
    grad_pre = contract_last(all_cot, down_weight) * slope
    grad_pre_low = grad_pre.astype(BF16)
    up_bias_part = jnp.sum(grad_pre, axis=0)
    grad_second = scatter_sum(contract_last(grad_pre_low, up_cols))
    outputs = (
        middle + scatter_sum(matmul(activated, down_weight)) + vectors[3]
    ).astype(BF16)

    down_part = contract_rows(activated, all_cot).astype(BF16)
    up_part = contract_rows(second_in, grad_pre_low).astype(BF16)
    up_rows = exchange(up_part.reshape(count, own, hidden))

    def reduce_dp(part, dim):
        share = lax.psum_scatter(part, "dp", scatter_dimension=dim, tiled=True)
        return lax.all_gather(share, "dp", axis=dim, tiled=True).astype(F32)

    down_weight_grad = reduce_dp(down_part, 0)
    up_rows = in_order([v[None] for v in up_rows])
    up_total = reduce_dp(up_rows.reshape(count * own, hidden), 0)
    up_weight_grad = (
        up_total.reshape(count, own, hidden).transpose(1, 0, 2).reshape(own, count * hidden)
    )

    grad_middle = cotangent[0].astype(F32) + norm_backward(
        grad_second, second_hat, second_inv, second_gain_full
    )
    grad_middle_low = grad_middle.astype(BF16)
    all_grad_middle = jnp.concatenate(gather(grad_middle_low), axis=0)
    grad_attended = contract_last(all_grad_middle, head_out).astype(BF16)
    grad_queries, grad_kv, head_sums = attention_backward(
        qkv, grad_attended, attended, logs, rows_info, cols_info, per
    )
    grad_qkv = jnp.concatenate([grad_queries, grad_kv], axis=1)
    grad_first = scatter_sum(contract_last(grad_qkv, qkv_cols))
    first_hat, first_inv = normalise(residual_in)
    input_grad = grad_middle + norm_backward(grad_first, first_hat, first_inv, first_gain_full)

    true_attended = in_order([v[None] for v in att_pieces])
    true_attended = true_attended.transpose(1, 0, 2).reshape(length, padded)[:, :model]
    own_features = jnp.concatenate(
        exchange(true_attended.reshape(length, count, own).transpose(1, 0, 2)), axis=0
    )
    out_part = contract_rows(own_features, all_grad_middle).astype(BF16)
    qkv_part = contract_rows(first_in, grad_qkv).astype(BF16)
    qkv_rows = exchange(qkv_part.reshape(count, own, 3 * width))
    qkv_rows = in_order([v[None] for v in qkv_rows]).reshape(count, own, 3, width)
    qkv_rows = qkv_rows.transpose(2, 1, 0, 3).reshape(3, own, padded)[:, :, :model]
    square = reduce_dp(jnp.concatenate([out_part[None], qkv_rows]).reshape(4 * own, model), 0)
    square = square.reshape(4, own, model)

    to_full = lambda v: lax.dynamic_update_slice(
        jnp.zeros((padded,), F32), v, (me * width,)
    )[:model]
    partials = jnp.stack(
        [
            to_full(head_sums[0]),
            to_full(head_sums[1]),
            jnp.sum(grad_middle, axis=0),
            jnp.sum(cotangent[0].astype(F32), axis=0),
            jnp.sum(grad_first * first_hat, axis=0),
            jnp.sum(grad_first, axis=0),
            jnp.sum(grad_second * second_hat, axis=0),
            jnp.sum(grad_second, axis=0),
        ]
    )
    vector_rows = sum(exchange(partials.reshape(8, count, own).transpose(1, 0, 2)))
    summed, up_bias_grad = lax.psum((vector_rows, up_bias_part), "dp")
    return (
        outputs[None],
        input_grad[None],
        square[1],
        square[2],
        square[3],
        square[0],
        up_weight_grad,
        down_weight_grad,
        summed[0],
        summed[1],
        summed[2],
        up_bias_grad,
        summed[3],
        summed[4],
        summed[5],
        summed[6],
        summed[7],
    )


def call(kernel, out_shape, out_specs, in_specs, scratch=(), grid=()):
    return pl.pallas_call(
        kernel,
        grid=grid,
        in_specs=in_specs,
        out_specs=out_specs,
        out_shape=out_shape,
        scratch_shapes=scratch,
    )


def assemble(pieces, slots, total):
    amount = len(pieces)
    shape = pieces[0].shape[-2:]

    def kernel(slot_ref, *refs):
        out_ref = refs[amount]
        at = 0
        for ref in refs[:amount]:
            parts = [ref[...]] if len(ref.shape) == 2 else [ref[k] for k in range(ref.shape[0])]
            for part in parts:
                out_ref[slot_ref[at]] = part
                at += 1

    return call(
        kernel,
        jax.ShapeDtypeStruct((total,) + shape, pieces[0].dtype),
        pl.BlockSpec(memory_space=pltpu.VMEM),
        [pl.BlockSpec(memory_space=pltpu.SMEM)]
        + [pl.BlockSpec(memory_space=pltpu.VMEM)] * amount,
    )(jnp.stack(slots).astype(jnp.int32), *pieces)


def grad_columns(first_in, grad_qkv, core, count):
    model = first_in.shape[1]
    full = grad_qkv.shape[1]
    own = model // count
    half = own // 2

    def kernel(core_ref, in_ref, grad_ref, keep_ref, give_ref, acc_ref):
        acc_ref[...] = contract_rows(in_ref[...], grad_ref[...])
        for j in range(count):
            for side, ref in enumerate((keep_ref, give_ref)):
                which = core_ref[0] if side == 0 else 1 - core_ref[0]
                start = pl.multiple_of(j * own + which * half, 8)
                ref[j] = acc_ref[pl.ds(start, half), :].astype(BF16)

    return call(
        kernel,
        [jax.ShapeDtypeStruct((count, half, full), BF16)] * 2,
        [pl.BlockSpec(memory_space=pltpu.VMEM)] * 2,
        [pl.BlockSpec(memory_space=pltpu.SMEM)] + [pl.BlockSpec(memory_space=pltpu.VMEM)] * 2,
        [pltpu.VMEM((model, full), F32)],
    )(core[None].astype(jnp.int32), first_in, grad_qkv)


def unfold(mine, theirs, core, near, far, mode):
    blocks = len(mine)
    half, model = mine[0].shape
    shapes = {
        "rows": [(2 * blocks, half, model)],
        "columns": [(2 * half, blocks * model)],
        "arrays": [(2 * half, model)] * blocks,
    }[mode]

    def kernel(bits_ref, *refs):
        out_refs = refs[2 * blocks :]
        mask = bits_ref[1] * 2 + bits_ref[2]
        for side in range(2):
            where = bits_ref[0] if side == 0 else 1 - bits_ref[0]
            rows = pl.ds(pl.multiple_of(where * half, 8), half)
            values = [refs[side * blocks + k][...] for k in range(blocks)]
            for slot in range(blocks):
                if mode == "rows":
                    out_refs[0][where * blocks + (slot ^ mask)] = values[slot].astype(F32)
                    continue
                block = values[slot]
                for k in range(1, blocks):
                    block = jnp.where(mask == k, values[slot ^ k], block)
                if mode == "columns":
                    out_refs[0][rows, slot * model : (slot + 1) * model] = block.astype(F32)
                else:
                    out_refs[slot][rows, :] = block.astype(F32)

    return call(
        kernel,
        [jax.ShapeDtypeStruct(shape, F32) for shape in shapes],
        [pl.BlockSpec(memory_space=pltpu.VMEM)] * len(shapes),
        [pl.BlockSpec(memory_space=pltpu.SMEM)]
        + [pl.BlockSpec(memory_space=pltpu.VMEM)] * (2 * blocks),
    )(jnp.stack([core, near, far]).astype(jnp.int32), *mine, *theirs)


def cut_columns(weights, me, core, count, wide):
    rows, _ = weights[0].shape
    half = rows // 2
    full = 3 * (wide + HD)

    def kernel(place_ref, *refs):
        outs = refs[3:]
        for k in range(count):
            start = pl.multiple_of((place_ref[0] ^ k) * wide, LANES)
            for m in range(3):
                main = refs[m][:, pl.ds(start, wide)]
                extra = refs[m][:, count * wide :]
                if k > 0:
                    main = jnp.where(place_ref[1] == 0, main[:half], main[half:])
                    extra = jnp.where(place_ref[1] == 0, extra[:half], extra[half:])
                outs[k][:, m * wide : (m + 1) * wide] = main
                outs[k][:, 3 * wide + m * HD : 3 * wide + (m + 1) * HD] = extra

    return call(
        kernel,
        [
            jax.ShapeDtypeStruct((rows if k == 0 else half, full), BF16)
            for k in range(count)
        ],
        [pl.BlockSpec(memory_space=pltpu.VMEM)] * count,
        [pl.BlockSpec(memory_space=pltpu.SMEM)] + [pl.BlockSpec(memory_space=pltpu.VMEM)] * 3,
    )(jnp.stack([me, core]).astype(jnp.int32), *weights)


def mid_forward(pieces, last, slots, wide, full_out, residual, rows):
    amount = len(pieces)
    length = pieces[0].shape[0]
    model = full_out.shape[0]

    def kernel(slot_ref, *refs):
        last_ref, weight_ref, res_ref, row_ref = refs[amount : amount + 4]
        att_ref, mid_ref, hat_ref, inv_ref, low_ref = refs[amount + 4 :]
        for k in range(amount):
            start = pl.multiple_of(slot_ref[k] * wide, LANES)
            att_ref[:, pl.ds(start, wide)] = refs[k][...]
        att_ref[:, amount * wide :] = last_ref[...]
        middle = res_ref[...].astype(F32) + matmul(att_ref[...], weight_ref[...]) + row_ref[0:1]
        mid_ref[...] = middle
        hat, inv_std = normalise(middle)
        hat_ref[...] = hat
        inv_ref[...] = jnp.broadcast_to(inv_std, (length, LANES))
        low_ref[...] = (hat * row_ref[1:2] + row_ref[2:3]).astype(BF16)

    shape = lambda width, kind: jax.ShapeDtypeStruct((length, width), kind)
    return call(
        kernel,
        [shape(model, BF16), shape(model, F32), shape(model, F32), shape(LANES, F32),
         shape(model, BF16)],
        [pl.BlockSpec(memory_space=pltpu.VMEM)] * 5,
        [pl.BlockSpec(memory_space=pltpu.SMEM)]
        + [pl.BlockSpec(memory_space=pltpu.VMEM)] * (amount + 4),
    )(jnp.stack(slots).astype(jnp.int32), *pieces, last, full_out, residual, rows)


def mid_backward(whole, pieces, hat, inv_std, cot, gain):
    length, model = hat.shape
    amount = len(pieces)

    def kernel(whole_ref, *refs):
        hat_ref, inv_ref, cot_ref, gain_ref = refs[amount : amount + 4]
        grad_ref, low_ref, sums_ref = refs[amount + 4 :]
        grad = whole_ref[...]
        for ref in refs[:amount]:
            grad = grad + ref[...].astype(F32)
        normed = hat_ref[...]
        cot_float = cot_ref[...].astype(F32)
        grad_mid = cot_float + norm_backward(grad, normed, inv_ref[:, 0:1], gain_ref[...])
        grad_ref[...] = grad_mid
        low_ref[...] = grad_mid.astype(BF16)
        total = lambda v: jnp.sum(v, axis=0, keepdims=True)
        sums_ref[0:1] = total(grad_mid)
        sums_ref[1:2] = total(cot_float)
        sums_ref[2:3] = total(grad * normed)
        sums_ref[3:4] = total(grad)
        sums_ref[4:8] = jnp.zeros((4, model), F32)

    flat = lambda rows, width: pl.BlockSpec((rows, width), lambda b: (0, 0))
    return call(
        kernel,
        [
            jax.ShapeDtypeStruct((length, model), F32),
            jax.ShapeDtypeStruct((length, model), BF16),
            jax.ShapeDtypeStruct((8, model), F32),
        ],
        [flat(length, model), flat(length, model), flat(8, model)],
        [flat(length, model)] * (amount + 2)
        + [flat(length, LANES), flat(length, model), flat(1, model)],
        grid=(1,),
    )(whole, *pieces, hat, inv_std, cot, gain[None])


def place_grads(out_part, pieces, slots, wide):
    amount = len(pieces)
    rows, model = out_part.shape

    def kernel(slot_ref, *refs):
        out_ref = refs[amount + 1]
        out_ref[0] = refs[0][...]
        for m in range(3):
            extra = slice(3 * wide + m * HD, 3 * wide + (m + 1) * HD)
            shared = refs[1][:, extra].astype(F32)
            for k in range(amount):
                start = pl.multiple_of(slot_ref[k] * wide, LANES)
                out_ref[1 + m, :, pl.ds(start, wide)] = refs[1 + k][:, m * wide : (m + 1) * wide]
                if k > 0:
                    shared = shared + refs[1 + k][:, extra].astype(F32)
            out_ref[1 + m, :, amount * wide :] = shared.astype(BF16)

    return call(
        kernel,
        jax.ShapeDtypeStruct((4, rows, model), BF16),
        pl.BlockSpec(memory_space=pltpu.VMEM),
        [pl.BlockSpec(memory_space=pltpu.SMEM)]
        + [pl.BlockSpec(memory_space=pltpu.VMEM)] * (amount + 1),
    )(jnp.stack(slots).astype(jnp.int32), out_part, *pieces)


def split_forward(qkv, rows_info, cols_info, heads, length):
    tokens = qkv.shape[0]
    wide = heads * HD
    block = min(256, tokens)
    full = qkv.shape[1]

    count = tokens // length
    piece = jax.ShapeDtypeStruct((length, wide), BF16)

    def kernel(q_ref, kv_ref, rows_ref, cols_ref, out_ref, last_ref, log_ref, *piece_refs):
        bias = mask_bias(
            rows_ref[:, 0:1], rows_ref[:, 1:2], cols_ref[0:1, :], cols_ref[1:2, :]
        )
        lane = lax.broadcasted_iota(jnp.int32, (block, LANES), 1)

        def head(query, keys, vals, seen):
            scores = contract_last(query, keys) * SCORE_SCALE + seen
            largest = jnp.max(scores, axis=1, keepdims=True)
            grown = jnp.exp(scores - largest)
            total = jnp.sum(grown, axis=1, keepdims=True)
            probs = (grown * (1.0 / total)).astype(BF16)
            return matmul(probs, vals).astype(BF16), largest + jnp.log(total)

        logs = jnp.zeros((block, LANES), F32)
        for h in range(heads):
            own = slice(h * HD, (h + 1) * HD)
            got, log = head(
                q_ref[:, own],
                kv_ref[:, wide + h * HD : wide + (h + 1) * HD],
                kv_ref[:, 2 * wide + h * HD : 2 * wide + (h + 1) * HD],
                bias,
            )
            out_ref[:, own] = got
            logs = jnp.where(lane == h, log, logs)
        log_ref[...] = logs

        @pl.when(pl.program_id(0) == 0)
        def _():
            base = 3 * wide
            got, log = head(
                q_ref[0:length, base : base + HD],
                kv_ref[:, base + HD : base + 2 * HD],
                kv_ref[:, base + 2 * HD : base + 3 * HD],
                bias[0:length],
            )
            last_ref[...] = got
            log_ref[0:length, :] = jnp.where(lane[0:length] == heads, log, logs[0:length])

        for k in range(1, count):
            at = k * length

            @pl.when(pl.program_id(0) == at // block)
            def _():
                piece_refs[k - 1][...] = out_ref[at % block : at % block + length, :]

    return call(
        kernel,
        [
            jax.ShapeDtypeStruct((tokens, wide), BF16),
            jax.ShapeDtypeStruct((length, HD), BF16),
            jax.ShapeDtypeStruct((tokens, LANES), F32),
        ]
        + [piece] * (count - 1),
        [
            pl.BlockSpec((block, wide), lambda b: (b, 0)),
            pl.BlockSpec((length, HD), lambda b: (0, 0)),
            pl.BlockSpec((block, LANES), lambda b: (b, 0)),
        ]
        + [pl.BlockSpec((length, wide), lambda b: (0, 0))] * (count - 1),
        [
            pl.BlockSpec((block, full), lambda b: (b, 0)),
            pl.BlockSpec((tokens, full), lambda b: (0, 0)),
            pl.BlockSpec((block, 2), lambda b: (b, 0)),
            pl.BlockSpec((2, tokens), lambda b: (0, 0)),
        ],
        grid=(tokens // block,),
    )(qkv, qkv, rows_info, cols_info)


def att_grads(pieces, head_out, last_out):
    amount = len(pieces)
    length, model = pieces[0].shape
    wide = head_out.shape[0]

    def kernel(*refs):
        head_ref, last_ref = refs[amount : amount + 2]
        all_ref, grad_ref, glast_ref = refs[amount + 2 :]
        for k in range(amount):
            rows = slice(k * length, (k + 1) * length)
            all_ref[rows, :] = refs[k][...]
        grad_ref[...] = contract_last(all_ref[...], head_ref[...]).astype(BF16)
        glast_ref[...] = contract_last(refs[0][...], last_ref[...]).astype(BF16)

    return call(
        kernel,
        [
            jax.ShapeDtypeStruct((amount * length, model), BF16),
            jax.ShapeDtypeStruct((amount * length, wide), BF16),
            jax.ShapeDtypeStruct((length, HD), BF16),
        ],
        [pl.BlockSpec(memory_space=pltpu.VMEM)] * 3,
        [pl.BlockSpec(memory_space=pltpu.VMEM)] * (amount + 2),
    )(*pieces, head_out, last_out)


def split_backward(qkv, grad_att, grad_last, attended, last, logs, rows_info, cols_info, heads):
    tokens, full = qkv.shape
    length = last.shape[0]
    wide = heads * HD
    block = min(256, tokens)
    steps = tokens // block
    base = 3 * wide

    def kernel(
        q_ref, kv_ref, grad_ref, glast_ref, att_ref, last_ref, log_ref, rows_ref, cols_ref,
        out_ref, sums_ref, acc_ref, bias_ref,
    ):
        step = pl.program_id(0)
        start = pl.multiple_of(step * block, block)

        @pl.when(step == 0)
        def _():
            acc_ref[...] = jnp.zeros_like(acc_ref)
            bias_ref[...] = jnp.zeros_like(bias_ref)
            out_ref[:, base : base + HD] = jnp.zeros((tokens, HD), BF16)

        seen = mask_bias(
            rows_ref[:, 0:1], rows_ref[:, 1:2], cols_ref[0:1, :], cols_ref[1:2, :]
        )

        def head(query, keys, vals, grad, got, log, bias):
            delta = jnp.sum(grad.astype(F32) * got.astype(F32), axis=1, keepdims=True)
            scores = contract_last(query, keys) * SCORE_SCALE + bias
            exact = jnp.exp(scores - log)
            grad_probs = contract_last(grad, vals)
            grad_scores = (exact * (grad_probs - delta) * SCORE_SCALE).astype(BF16)
            return (
                matmul(grad_scores, keys),
                contract_rows(grad_scores, query),
                contract_rows(exact.astype(BF16), grad),
            )

        for h in range(heads):
            own = slice(h * HD, (h + 1) * HD)
            keys_at = slice(wide + h * HD, wide + (h + 1) * HD)
            vals_at = slice(2 * wide + h * HD, 2 * wide + (h + 1) * HD)
            grad_query, grad_key, grad_value = head(
                q_ref[:, own], kv_ref[:, keys_at], kv_ref[:, vals_at],
                grad_ref[:, own], att_ref[:, own], log_ref[:, h : h + 1], seen,
            )
            out_ref[pl.ds(start, block), own] = grad_query.astype(BF16)
            bias_ref[0:1, own] += jnp.sum(grad_query, axis=0, keepdims=True)
            acc_ref[:, own] += grad_key
            acc_ref[:, keys_at] += grad_value

        @pl.when(step == 0)
        def _():
            grad_query, grad_key, grad_value = head(
                q_ref[0:length, base : base + HD],
                kv_ref[:, base + HD : base + 2 * HD],
                kv_ref[:, base + 2 * HD : base + 3 * HD],
                glast_ref[...], last_ref[...], log_ref[0:length, heads : heads + 1],
                seen[0:length],
            )
            out_ref[0:length, base : base + HD] = grad_query.astype(BF16)
            out_ref[:, base + HD : base + 2 * HD] = grad_key.astype(BF16)
            out_ref[:, base + 2 * HD : base + 3 * HD] = grad_value.astype(BF16)
            bias_ref[0:1, wide : wide + HD] = jnp.sum(grad_query, axis=0, keepdims=True)
            bias_ref[1:2, wide : wide + HD] = jnp.sum(grad_value, axis=0, keepdims=True)

        @pl.when(step == steps - 1)
        def _():
            out_ref[:, wide:base] = acc_ref[...].astype(BF16)
            bias_ref[1:2, 0:wide] = jnp.sum(acc_ref[:, wide:], axis=0, keepdims=True)
            sums_ref[...] = bias_ref[...]

    return call(
        kernel,
        [
            jax.ShapeDtypeStruct((tokens, full), BF16),
            jax.ShapeDtypeStruct((8, wide + HD), F32),
        ],
        [
            pl.BlockSpec((tokens, full), lambda b: (0, 0)),
            pl.BlockSpec((8, wide + HD), lambda b: (0, 0)),
        ],
        [
            pl.BlockSpec((block, full), lambda b: (b, 0)),
            pl.BlockSpec((tokens, full), lambda b: (0, 0)),
            pl.BlockSpec((block, wide), lambda b: (b, 0)),
            pl.BlockSpec((length, HD), lambda b: (0, 0)),
            pl.BlockSpec((block, wide), lambda b: (b, 0)),
            pl.BlockSpec((length, HD), lambda b: (0, 0)),
            pl.BlockSpec((block, LANES), lambda b: (b, 0)),
            pl.BlockSpec((block, 2), lambda b: (b, 0)),
            pl.BlockSpec((2, tokens), lambda b: (0, 0)),
        ],
        [pltpu.VMEM((tokens, 2 * wide), F32), pltpu.VMEM((8, wide + HD), F32)],
        grid=(steps,),
    )(qkv, qkv, grad_att, grad_last, attended, last, logs, rows_info, cols_info)


def on_device_paired(
    count,
    inputs,
    segment,
    cotangent,
    query_weight,
    key_weight,
    value_weight,
    out_weight,
    up_weight,
    down_weight,
    query_bias,
    value_bias,
    out_bias,
    up_bias,
    down_bias,
    first_gain,
    first_shift,
    second_gain,
    second_shift,
):
    me = lax.axis_index("shard")
    copy_index = lax.axis_index("dp")
    core = copy_index & 1
    near = (copy_index >> 1) & 1
    far = (copy_index >> 2) & 1
    others = range(1, count)
    order = me ^ jnp.arange(count, dtype=jnp.int32)
    slots = [me ^ k for k in range(count)]
    length = inputs.shape[1]
    model = inputs.shape[2]
    own = query_weight.shape[0]
    half = own // 2
    hidden = down_weight.shape[0]
    heads = HEADS // count
    wide = heads * HD
    full = 3 * (wide + HD)

    def send(value, k):
        return lax.ppermute(value, "shard", [(j, j ^ k) for j in range(count)])

    def cross(value, k):
        return lax.ppermute(value, "dp", [(j, j ^ k) for j in range(8)])

    def gather(value):
        return [value] + [send(value, k) for k in others]

    def pick(value, index):
        return lax.dynamic_index_in_dim(value, index, 0, False)

    def added(left, right):
        return (left.astype(F32) + right.astype(F32)).astype(BF16)

    def scatter_sum(partial_rows):
        total = partial_rows[0:length]
        for k in others:
            piece = partial_rows[k * length : (k + 1) * length].astype(BF16)
            total = total + send(piece, k).astype(F32)
        return total

    def rows_of_core(value, which):
        return lax.dynamic_slice_in_dim(value, which * half, half, axis=value.ndim - 2)

    def fetch(cuts, hold=None):
        got = [send(cuts[k], k) for k in others]
        if hold is not None:
            got = list(lax.optimization_barrier((*got, hold)))[:-1]
        swapped = [cross(g, 1) for g in got]
        pieces, places = [], []
        for k in others:
            pieces += [got[k - 1], swapped[k - 1]]
            places += [2 * slots[k] + core, 2 * slots[k] + 1 - core]
        pieces.append(cuts[0].reshape(2, half, -1))
        places += [2 * me, 2 * me + 1]
        return assemble(pieces, places, 2 * count)

    vectors = jnp.stack(
        [
            query_bias, value_bias, out_bias, down_bias,
            first_gain, first_shift, second_gain, second_shift,
        ]
    )
    input_pieces = gather(inputs[0])
    vector_pieces = gather(vectors)
    all_inputs = jnp.concatenate(input_pieces, axis=0)
    vectors = jnp.stack(vector_pieces)[order].transpose(1, 0, 2).reshape(8, model).astype(F32)

    squares = (query_weight, key_weight, value_weight)
    qkv_cols = fetch(cut_columns(squares, me, core, count, wide)).reshape(model, full)
    cot_pieces = gather(cotangent[0])
    all_cot = jnp.concatenate(cot_pieces, axis=0)

    pos = (order[:, None] * length + jnp.arange(length, dtype=jnp.int32)[None, :]).reshape(-1)
    seg = segment[0].reshape(count, length)[order].reshape(-1)
    rows_info = jnp.stack([seg, pos], axis=1)
    cols_info = jnp.stack([seg, pos], axis=0)

    head_slice = lambda v: lax.dynamic_slice_in_dim(v, me * wide, wide)
    tail = lambda v: v[count * wide :]
    qkv_bias = jnp.concatenate(
        [
            head_slice(vectors[0]), jnp.zeros((wide,), F32), head_slice(vectors[1]),
            tail(vectors[0]), jnp.zeros((HD,), F32), tail(vectors[1]),
        ]
    )

    first_gain_full, first_shift_full = vectors[4], vectors[5]
    second_gain_full, second_shift_full = vectors[6], vectors[7]
    all_hat, _ = normalise(all_inputs.astype(F32))
    first_in = (all_hat * first_gain_full + first_shift_full).astype(BF16)
    qkv = (matmul(first_in, qkv_cols) + qkv_bias).astype(BF16)
    out_half = rows_of_core(out_weight, core)
    full_out = fetch([out_weight] + [out_half] * 3, qkv).reshape(model, model)
    head_out = lax.dynamic_slice_in_dim(full_out, me * wide, wide, axis=0)
    last_out = full_out[count * wide :]
    attended, last, logs, *others_rows = split_forward(qkv, rows_info, cols_info, heads, length)
    att_pieces = [attended[0:length]] + [send(others_rows[k - 1], k) for k in others]
    stacked_up = jnp.stack([up_weight[:, j * hidden : (j + 1) * hidden] for j in range(count)])
    up_halves = rows_of_core(stacked_up, core)
    up_cuts = [pick(stacked_up, me)] + [pick(up_halves, slots[k]) for k in others]
    up_cols = fetch(up_cuts, attended).reshape(model, hidden)
    own_attended, middle, second_hat, second_inv, own_second_in = mid_forward(
        att_pieces, last, slots, wide, full_out, inputs[0],
        jnp.stack([vectors[2], second_gain_full, second_shift_full]),
    )
    residual_in = inputs[0].astype(F32)
    second_in = jnp.concatenate(gather(own_second_in), axis=0)
    pre_act = matmul(second_in, up_cols) + up_bias.astype(F32)
    below = 0.5 * (1.0 + lax.erf(pre_act * (0.5**0.5)))
    activated = (pre_act * below).astype(BF16)
    slope = below + pre_act * (jnp.exp(-0.5 * pre_act * pre_act) * 0.3989422804014327)
    grad_pre = contract_last(all_cot, down_weight) * slope
    grad_pre_low = grad_pre.astype(BF16)
    up_bias_part = jnp.sum(grad_pre, axis=0)
    second_rows = contract_last(grad_pre_low, up_cols)
    second_pieces = [
        send(second_rows[k * length : (k + 1) * length].astype(BF16), k) for k in others
    ]

    def reduce_far(part, mode):
        keep = lax.dynamic_slice_in_dim(part, 2 * near, 2, axis=0)
        give = lax.dynamic_slice_in_dim(part, 2 - 2 * near, 2, axis=0)
        pair = added(keep, cross(give, 2))
        one = added(pick(pair, far), cross(pick(pair, 1 - far), 4))
        back = cross(one, 4)
        mine = [one, back, cross(one, 2), cross(back, 2)]
        theirs = [cross(v, 1) for v in mine]
        return unfold(mine, theirs, core, near, far, mode), one

    down_part = contract_rows(activated, all_cot).astype(BF16)
    down_part = down_part.reshape(2, 4, hidden // 8, model)
    down_given = cross(pick(down_part, 1 - core), 1)
    down_half = added(pick(down_part, core), down_given)
    (down_sum,), _ = reduce_far(down_half, "rows")
    down_weight_grad = down_sum.reshape(hidden, model)

    up_part = contract_rows(second_in, grad_pre_low).astype(BF16)
    up_part = up_part.reshape(count, own, hidden)
    up_given = cross(rows_of_core(up_part, 1 - core), 1)
    up_part = added(rows_of_core(up_part, core), up_given)
    up_pieces = [pick(up_part, me)] + [send(pick(up_part, slots[k]), k) for k in others]
    grad_middle, grad_middle_low, mid_sums = mid_backward(
        second_rows, second_pieces, second_hat, second_inv, cotangent[0], second_gain_full
    )
    all_grad_middle, grad_attended, grad_last = att_grads(
        gather(grad_middle_low), head_out, last_out
    )
    grad_qkv, head_sums = split_backward(
        qkv, grad_attended, grad_last, attended, last, logs, rows_info, cols_info, heads
    )
    up_pieces = list(lax.optimization_barrier((*up_pieces, head_sums)))[:-1]
    (up_weight_grad,), up_one = reduce_far(assemble(up_pieces, slots, count), "columns")
    qkv_keep, qkv_give = grad_columns(first_in, grad_qkv, core, count)
    qkv_part = added(qkv_keep, cross(qkv_give, 1))
    late_qkv, _ = lax.optimization_barrier((grad_qkv, qkv_part))
    first_rows = contract_last(late_qkv, qkv_cols)
    first_pieces = [send(first_rows[k * length : (k + 1) * length].astype(BF16), k) for k in others]
    features = jnp.stack([own_attended[:, j * own : (j + 1) * own] for j in range(count)])
    feature_pieces = [send(pick(features, slots[k]), k) for k in others]
    *feature_pieces, _ = lax.optimization_barrier((*feature_pieces, qkv_give))
    own_features = jnp.concatenate([pick(features, me)] + feature_pieces, axis=0)
    out_part = contract_rows(own_features, all_grad_middle).astype(BF16)
    out_part = added(rows_of_core(out_part, core), cross(rows_of_core(out_part, 1 - core), 1))
    qkv_pieces = [pick(qkv_part, me)] + [send(pick(qkv_part, slots[k]), k) for k in others]
    placed = place_grads(out_part, qkv_pieces, slots, wide)
    *first_pieces, _ = lax.optimization_barrier((*first_pieces, placed))
    grad_first = sum((v.astype(F32) for v in first_pieces), first_rows[0:length])
    first_hat, first_inv = normalise(residual_in)
    input_grad = grad_middle + norm_backward(grad_first, first_hat, first_inv, first_gain_full)
    square, _ = reduce_far(placed, "arrays")
    late_activated, _ = lax.optimization_barrier((activated, up_one))
    output_rows = matmul(late_activated, down_weight)
    outputs = (middle + scatter_sum(output_rows) + vectors[3]).astype(BF16)

    def to_full(row):
        main = lax.dynamic_update_slice(
            jnp.zeros((count * wide,), F32), row[:wide], (me * wide,)
        )
        return jnp.concatenate([main, row[wide:]])

    partials = jnp.stack(
        [
            to_full(head_sums[0]),
            to_full(head_sums[1]),
            mid_sums[0],
            mid_sums[1],
            jnp.sum(grad_first * first_hat, axis=0),
            jnp.sum(grad_first, axis=0),
            mid_sums[2],
            mid_sums[3],
        ]
    )
    rows = partials.reshape(8, count, own).transpose(1, 0, 2)
    mine = pick(rows, me)
    for k in others:
        mine = mine + send(pick(rows, slots[k]), k)
    summed = jnp.concatenate([mine, up_bias_part.reshape(count, own)], axis=0)
    for k in (1, 2, 4):
        summed = summed + cross(summed, k)
    return (
        outputs[None],
        input_grad[None],
        square[1],
        square[2],
        square[3],
        square[0],
        up_weight_grad,
        down_weight_grad,
        summed[0],
        summed[1],
        summed[2],
        summed[8:].reshape(hidden),
        summed[3],
        summed[4],
        summed[5],
        summed[6],
        summed[7],
    )


def on_device(count, copies, *args):
    model = args[0].shape[2]
    heads = HEADS // count
    paired = (
        count == 4
        and copies == 8
        and HEADS == count * heads + 1
        and (heads * HD) % LANES == 0
        and model % (count * 16) == 0
        and args[0].shape[1] <= 256
        and args[8].shape[0] == model
    )
    if paired:
        return on_device_paired(count, *args)
    return on_device_general(count, *args)


def solution(mesh):
    tokens = P("dp", "shard", None)
    matrix = P("shard", None)
    vector = P("shard")
    return jax.shard_map(
        partial(on_device, mesh.shape["shard"], mesh.shape["dp"]),
        mesh=mesh,
        in_specs=(tokens, P("dp", None), tokens) + (matrix,) * 6 + (vector,) * 9,
        out_specs=(tokens, tokens) + (matrix,) * 6 + (vector,) * 9,
        check_vma=False,
    )
```

profile of v0, /device:TPU:5, one launch (start us, length us, event | category | flops | bytes accessed | tf_op | source)
XLA Modules:
  0.0 414.9 jit_solution(3250887643284565009)
XLA Ops:
  14.6 3.8 slice_bitcast_fusion.3
  28.4 2.7 shard_map.305
  34.9 9.4 %collective-permute-done.6.refs_0_ = bf16[136,960]{1,0:T(8,128)(2,1)} collective-permute-done((bf16[136,960]{1,0:T(8,128)(2,1)}, bf16[136,960]{1,0:T(8,128)(2,1)}, u32[]{:S(2)}, u32[]{:S(2)}) %collective-permute-start.6) | collective-permute-done | bytes 261152 | tf_op jit(solution)/shard_map/ppermute | solution.py:845
  47.4 3.5 collective-permute-done.10.refs_4_
  51.2 7.4 %collective-permute-start.7 = (bf16[136,960]{1,0:T(8,128)(2,1)}, bf16[136,960]{1,0:T(8,128)(2,1)S(1)}, u32[]{:S(2)}, u32[]{:S(2)}) collective-permute-start(bf16[136,960]{1,0:T(8,128)(2,1)} %collective-permute-done.6.refs_0_), channel_id=1, source_target_pairs={{0,1},{1,0},{2,3},{3,2},{4,5},{5,4},{6,7},{7,6},{8,9},{9,8},{10,11... | collective-permute-start | bytes 783368 | tf_op jit(solution)/shard_map/ppermute | solution.py:848
  61.7 2.5 fusion.6.in_ref
  67.6 3.1 shard_map.306
  70.7 4.6 %add_convert_fusion.2.q_ref.kv_ref = bf16[512,960]{1,0:T(8,128)(2,1)} fusion(bf16[512,1088]{1,0:T(8,128)(2,1)} %fusion.6.in_ref, bf16[1088,960]{1,0:T(8,128)(2,1)} %bitcast.174, f32[960]{0:T(1024)S(1)} %concatenate.26), kind=kOutput, calls=%fused_computation.27 | convolution fusion | flops 1070530560 | bytes 4189952 | tf_op jit(solution)/shard_map/dot_general | solution.py:40
  78.3 2.9 collective-permute-done.24.refs_0_
  83.3 8.2 %shard_map.307 = (bf16[512,256]{1,0:T(8,128)(2,1)}, bf16[128,64]{1,0:T(8,128)(2,1)}, f32[512,128]{1,0:T(8,128)}, bf16[128,256]{1,0:T(8,128)(2,1)}, bf16[128,256]{1,0:T(8,128)(2,1)}, /*index=5*/bf16[128,256]{1,0:T(8,128)(2,1)}) custom-call(bf16[512,960]{1,0:T(8,128)(2,1)} %add_convert_fusion.2.q_ref.kv_ref, bf16[512,960]{1,0:T(8,128)(2,1)} %add_convert_fusion.2.q_ref.kv_ref, ...), custom_call_target="tpu_custom_call" | custom-call | tf_op jit(solution)/shard_map/pallas_call | solution.py:659
  97.9 3.3 shard_map.308
  102.3 3.6 shard_map.309
  113.6 2.4 collective-permute-start.32
  116.4 3.3 shard_map.310
  125.8 9.4 %collective-permute-done.23 = bf16[128,1088]{1,0:T(8,128)(2,1)S(1)} collective-permute-done((bf16[128,1088]{1,0:T(8,128)(2,1)S(1)}, bf16[128,1088]{1,0:T(8,128)(2,1)S(1)}, u32[]{:S(2)}, u32[]{:S(2)}) %collective-permute-start.23) | collective-permute-done | bytes 278560 | tf_op jit(solution)/shard_map/ppermute | solution.py:845
  137.4 5.0 %multiply_convert_fusion = (bf16[512,1088]{0,1:T(8,128)(2,1)}, f32[512,1088]{0,1:T(8,128)S(1)}) fusion(f32[1088]{0:T(1024)S(1)} %copy-done.48, bf16[512,1088]{1,0:T(8,128)(2,1)} %constant_dynamic-update-slice_fusion, bf16[1088,1088]{1,0:T(8,128)(2,1)} %bitcast.168), kind=kOutput, calls=%fused_computation.25 | convolution fusion | flops 1215496192 | bytes 6828288 | tf_op jit(solution)/shard_map/dot_general | solution.py:40
  142.4 3.6 fusion.60
  146.1 3.2 convolution_convert_fusion.1
  149.3 3.3 fusion.57
  156.2 4.7 %convolution_convert_fusion = bf16[1088,1088]{1,0:T(8,128)(2,1)} fusion(bf16[512,1088]{0,1:T(8,128)(2,1)} %get-tuple-element.92, bf16[128,1088]{1,0:T(8,128)(2,1)} %collective-permute-done.32, bf16[128,1088]{1,0:T(8,128)(2,1)} %collective-permute-done.31, bf16[128,1088]{1,0:T(8,128)(2,1)} %collective-permute-done.30, bf16[128,1088]{1,0:T(8,128)(2,1)S(1)} %bitcast.182), kind=kOutput, calls=%fused_computation.2 | convolution fusion | flops 1217794048 | bytes 4595712 | tf_op jit(solution)/shard_map/dot_general | solution.py:44
  165.4 3.2 shard_map.311
  170.0 2.4 dynamic-slice_bitcast_fusion
  174.4 2.4 collective-permute-start.42
  180.4 7.3 %collective-permute-start.33 = (bf16[4,136,1088]{2,1,0:T(8,128)(2,1)}, bf16[4,136,1088]{2,1,0:T(8,128)(2,1)}, u32[]{:S(2)}, u32[]{:S(2)}) collective-permute-start(bf16[4,136,1088]{2,1,0:T(8,128)(2,1)} %constant_dynamic-slice_fusion.9), channel_id=1, source_target_pairs={{0,1},{1,0},{2,3},{3,2},{4,5},{5,4},{6,7},{7,6},{8,9},{9,8},{10,11... | collective-permute-start | bytes 3551240 | tf_op jit(solution)/shard_map/ppermute | solution.py:848
  187.8 4.9 %collective-permute-start.75 = (bf16[4,136,1088]{2,1,0:T(8,128)(2,1)}, bf16[4,136,1088]{2,1,0:T(8,128)(2,1)}, u32[]{:S(2)}, u32[]{:S(2)}) collective-permute-start(bf16[4,136,1088]{2,1,0:T(8,128)(2,1)} %dynamic-slice_bitcast_fusion), channel_id=1, source_target_pairs={{0,1},{1,0},{2,3},{3,2},{4,5},{5,4},{6,7},{7,6},{8,9},{9,8},{10,11... | collective-permute-start | bytes 3551240 | tf_op jit(solution)/shard_map/ppermute | solution.py:848
  192.7 3.0 shard_map.312
  195.7 9.1 %shard_map.313 = (bf16[512,960]{1,0:T(8,128)(2,1)}, f32[8,320]{1,0:T(8,128)}) custom-call(bf16[512,960]{1,0:T(8,128)(2,1)} %add_convert_fusion.2.q_ref.kv_ref, bf16[512,960]{1,0:T(8,128)(2,1)} %add_convert_fusion.2.q_ref.kv_ref, bf16[512,256]{1,0:T(8,128)(2,1)} %get-tuple-element.84.grad_ref, bf16[128,64]{1,0:T(8,128)(2,1)} %get-tuple-element.85.glast_ref, ...), custom_call_target="tpu_custom_call" | custom-call | tf_op jit(solution)/shard_map/pallas_call | solution.py:780
  204.8 4.5 %shard_map.315 = (bf16[4,136,960]{2,1,0:T(8,128)(2,1)}, bf16[4,136,960]{2,1,0:T(8,128)(2,1)}) custom-call(s32[1]{0:T(128)} %bitcast.19.core_ref, bf16[512,1088]{1,0:T(8,128)(2,1)} %fusion.6.in_ref, bf16[512,960]{1,0:T(8,128)(2,1)} %get-tuple-element.97.grad_ref), custom_call_target="tpu_custom_call" | custom-call | tf_op jit(solution)/shard_map/pallas_call | solution.py:436
  226.2 3.0 fusion.59
  231.7 3.7 collective-permute-done.35.refs_2_
  235.6 4.9 %collective-permute-done.56.refs_2_ = bf16[136,960]{1,0:T(8,128)(2,1)S(1)} collective-permute-done((bf16[136,960]{1,0:T(8,128)(2,1)S(1)}, bf16[136,960]{1,0:T(8,128)(2,1)S(1)}, u32[]{:S(2)}, u32[]{:S(2)}) %collective-permute-start.56) | collective-permute-done | bytes 261152 | tf_op jit(solution)/shard_map/ppermute | solution.py:845
  246.1 14.0 %collective-permute-done.57.refs_3_ = bf16[136,960]{1,0:T(8,128)(2,1)} collective-permute-done((bf16[136,960]{1,0:T(8,128)(2,1)}, bf16[136,960]{1,0:T(8,128)(2,1)}, u32[]{:S(2)}, u32[]{:S(2)}) %collective-permute-start.57) | collective-permute-done | bytes 261152 | tf_op jit(solution)/shard_map/ppermute | solution.py:845
  261.6 2.5 shard_map.316
  264.1 2.9 fusion.24
  270.1 4.9 %collective-permute-done.76 = bf16[2,136,1088]{2,1,0:T(8,128)(2,1)} collective-permute-done((bf16[2,136,1088]{2,1,0:T(8,128)(2,1)}, bf16[2,136,1088]{2,1,0:T(8,128)(2,1)}, u32[]{:S(2)}, u32[]{:S(2)}) %collective-permute-start.76) | collective-permute-done | bytes 591904 | tf_op jit(solution)/shard_map/ppermute | solution.py:848
  276.4 3.7 collective-permute-start.88
  284.2 11.4 %collective-permute-done.89 = f32[12,272]{1,0:T(8,128)S(1)} collective-permute-done((f32[12,272]{1,0:T(8,128)S(1)}, f32[12,272]{1,0:T(8,128)S(1)}, u32[]{:S(2)}, u32[]{:S(2)}) %collective-permute-start.89) | collective-permute-done | bytes 13088 | tf_op jit(solution)/shard_map/ppermute | solution.py:848
  302.9 12.4 %collective-permute-done.44 = bf16[136,1088]{1,0:T(8,128)(2,1)S(1)} collective-permute-done((bf16[136,1088]{1,0:T(8,128)(2,1)S(1)}, bf16[136,1088]{1,0:T(8,128)(2,1)S(1)}, u32[]{:S(2)}, u32[]{:S(2)}) %collective-permute-start.44) | collective-permute-done | bytes 295968 | tf_op jit(solution)/shard_map/ppermute | solution.py:848
  315.4 11.1 %collective-permute-start.81 = (bf16[136,1088]{1,0:T(8,128)(2,1)}, bf16[136,1088]{1,0:T(8,128)(2,1)}, u32[]{:S(2)}, u32[]{:S(2)}) collective-permute-start(bf16[136,1088]{1,0:T(8,128)(2,1)} %fusion.16.refs_0_), channel_id=1, source_target_pairs={{0,1},{1,0},{2,3},{3,2},{4,5},{5,4},{6,7},{7,6},{8,9},{9,8},{10,11... | collective-permute-start | bytes 887816 | tf_op jit(solution)/shard_map/ppermute | solution.py:848
  327.2 3.3 fusion.58
  336.2 6.0 %collective-permute-done.47 = bf16[128,1088]{1,0:T(8,128)(2,1)} collective-permute-done((bf16[128,1088]{1,0:T(8,128)(2,1)}, bf16[128,1088]{1,0:T(8,128)(2,1)}, u32[]{:S(2)}, u32[]{:S(2)}) %collective-permute-start.47) | collective-permute-done | bytes 278560 | tf_op jit(solution)/shard_map/ppermute | solution.py:845
  342.2 12.0 %collective-permute-done.60 = bf16[136,1088]{1,0:T(8,128)(2,1)} collective-permute-done((bf16[136,1088]{1,0:T(8,128)(2,1)}, bf16[136,1088]{1,0:T(8,128)(2,1)}, u32[]{:S(2)}, u32[]{:S(2)}) %collective-permute-start.60) | collective-permute-done | bytes 295968 | tf_op jit(solution)/shard_map/ppermute | solution.py:848
  356.1 6.6 %collective-permute-done.45 = bf16[128,1088]{1,0:T(8,128)(2,1)S(1)} collective-permute-done((bf16[128,1088]{1,0:T(8,128)(2,1)}, bf16[128,1088]{1,0:T(8,128)(2,1)S(1)}, u32[]{:S(2)}, u32[]{:S(2)}) %collective-permute-start.45) | collective-permute-done | bytes 278560 | tf_op jit(solution)/shard_map/ppermute | solution.py:845
  368.7 12.0 %collective-permute-done.70.refs_3_ = bf16[136,1088]{1,0:T(8,128)(2,1)S(1)} collective-permute-done((bf16[136,1088]{1,0:T(8,128)(2,1)}, bf16[136,1088]{1,0:T(8,128)(2,1)S(1)}, u32[]{:S(2)}, u32[]{:S(2)}) %collective-permute-start.70) | collective-permute-done | bytes 295968 | tf_op jit(solution)/shard_map/ppermute | solution.py:848
  391.8 4.5 %collective-permute-done.63.refs_3_ = bf16[136,1088]{1,0:T(8,128)(2,1)} collective-permute-done((bf16[136,1088]{1,0:T(8,128)(2,1)}, bf16[136,1088]{1,0:T(8,128)(2,1)}, u32[]{:S(2)}, u32[]{:S(2)}) %collective-permute-start.63) | collective-permute-done | bytes 295968 | tf_op jit(solution)/shard_map/ppermute | solution.py:848
  400.1 4.3 %shard_map.319 = f32[8,136,1088]{2,1,0:T(8,128)} custom-call(s32[3]{0:T(128)} %pad_add_fusion.4.bits_ref, bf16[136,1088]{1,0:T(8,128)(2,1)} %fusion.16.refs_0_, bf16[136,1088]{1,0:T(8,128)(2,1)} %collective-permute-done.78.refs_1_, bf16[136,1088]{1,0:T(8,128)(2,1)} %collective-permute-done.79.refs_2_, bf16[136,1088]{1,0:T(8,128)(2,1)} %collective-permute-done.80.refs_3_, ...), custom_call_target="tpu_custom_call" | custom-call | tf_op jit(solution)/shard_map/pallas_call | solution.py:473
  405.2 4.6 %shard_map.318 = f32[272,4352]{1,0:T(8,128)} custom-call(s32[3]{0:T(128)} %pad_add_fusion.4.bits_ref, bf16[136,1088]{1,0:T(8,128)(2,1)} %fusion.18.refs_0_, bf16[136,1088]{1,0:T(8,128)(2,1)} %collective-permute-done.68.refs_1_, bf16[136,1088]{1,0:T(8,128)(2,1)} %collective-permute-done.69.refs_2_, bf16[136,1088]{1,0:T(8,128)(2,1)} %copy-done.15, ...), custom_call_target="tpu_custom_call" | custom-call | tf_op jit(solution)/shard_map/pallas_call | solution.py:473
  410.4 4.3 %shard_map.317 = (f32[272,1088]{1,0:T(8,128)}, f32[272,1088]{1,0:T(8,128)}, f32[272,1088]{1,0:T(8,128)}, f32[272,1088]{1,0:T(8,128)}) custom-call(s32[3]{0:T(128)} %pad_add_fusion.4.bits_ref, bf16[136,1088]{1,0:T(8,128)(2,1)} %fusion.17.refs_0_, bf16[136,1088]{1,0:T(8,128)(2,1)} %collective-permute-done.61.refs_1_, ...), custom_call_target="tpu_custom_call" | custom-call | tf_op jit(solution)/shard_map/pallas_call | solution.py:473
  (409 shorter events, 154.3 us)
Async XLA Ops:
  6.3 25.4 %collective-permute-start.5 = (bf16[8,272]{1,0:T(8,128)(2,1)S(1)}, bf16[8,272]{1,0:T(8,128)(2,1)S(1)}, u32[]{:S(2)}, u32[]{:S(2)}) collective-permute-start(bf16[8,272]{1,0:T(8,128)(2,1)S(1)} %stack.209), channel_id=1, source_target_pairs={{0,24},{8,16},{16,8},{24,0},{1,25},{9,17},{17,9},{25,1},{2,26},{10... | collective-permute-start | bytes 13064 | tf_op jit(solution)/shard_map/ppermute | solution.py:845
  7.5 24.5 %collective-permute-start.4 = (bf16[8,272]{1,0:T(8,128)(2,1)S(1)}, bf16[8,272]{1,0:T(8,128)(2,1)S(1)}, u32[]{:S(2)}, u32[]{:S(2)}) collective-permute-start(bf16[8,272]{1,0:T(8,128)(2,1)S(1)} %stack.209), channel_id=1, source_target_pairs={{0,16},{8,24},{16,0},{24,8},{1,17},{9,25},{17,1},{25,9},{2,18},{10... | collective-permute-start | bytes 13064 | tf_op jit(solution)/shard_map/ppermute | solution.py:845
  8.8 24.4 %collective-permute-start.3 = (bf16[8,272]{1,0:T(8,128)(2,1)S(1)}, bf16[8,272]{1,0:T(8,128)(2,1)S(1)}, u32[]{:S(2)}, u32[]{:S(2)}) collective-permute-start(bf16[8,272]{1,0:T(8,128)(2,1)S(1)} %stack.209), channel_id=1, source_target_pairs={{0,8},{8,0},{16,24},{24,16},{1,9},{9,1},{17,25},{25,17},{2,10},{10... | collective-permute-start | bytes 13064 | tf_op jit(solution)/shard_map/ppermute | solution.py:845
  10.2 41.0 %collective-permute-start.2 = (bf16[128,1088]{1,0:T(8,128)(2,1)S(1)}, bf16[128,1088]{1,0:T(8,128)(2,1)S(1)}, u32[]{:S(2)}, u32[]{:S(2)}) collective-permute-start(bf16[128,1088]{1,0:T(8,128)(2,1)S(1)} %bitcast.156), channel_id=1, source_target_pairs={{0,24},{8,16},{16,8},{24,0},{1,25},{9,17},{17,9},{25,1},{2,26},{10... | collective-permute-start | bytes 835592 | tf_op jit(solution)/shard_map/ppermute | solution.py:845
  11.4 47.2 %collective-permute-start.1 = (bf16[128,1088]{1,0:T(8,128)(2,1)S(1)}, bf16[128,1088]{1,0:T(8,128)(2,1)S(1)}, u32[]{:S(2)}, u32[]{:S(2)}) collective-permute-start(bf16[128,1088]{1,0:T(8,128)(2,1)S(1)} %bitcast.157), channel_id=1, source_target_pairs={{0,16},{8,24},{16,0},{24,8},{1,17},{9,25},{17,1},{25,9},{2,18},{10... | collective-permute-start | bytes 835592 | tf_op jit(solution)/shard_map/ppermute | solution.py:845
  31.7 26.9 %collective-permute-start = (bf16[128,1088]{1,0:T(8,128)(2,1)S(1)}, bf16[128,1088]{1,0:T(8,128)(2,1)}, u32[]{:S(2)}, u32[]{:S(2)}) collective-permute-start(bf16[128,1088]{1,0:T(8,128)(2,1)S(1)} %bitcast.158), channel_id=1, source_target_pairs={{0,8},{8,0},{16,24},{24,16},{1,9},{9,1},{17,25},{25,17},{2,10},{10... | collective-permute-start | bytes 835592 | tf_op jit(solution)/shard_map/ppermute | solution.py:845
  46.4 28.9 %collective-permute-start.15 = (bf16[136,1088]{1,0:T(8,128)(2,1)}, bf16[136,1088]{1,0:T(8,128)(2,1)}, u32[]{:S(2)}, u32[]{:S(2)}) collective-permute-start(bf16[136,1088]{1,0:T(8,128)(2,1)} %constant_dynamic-slice_fusion.11), channel_id=1, source_target_pairs={{0,8},{8,0},{16,24},{24,16},{1,9},{9,1},{17,25},{25,17},{2,10},{10... | collective-permute-start | bytes 887816 | tf_op jit(solution)/shard_map/ppermute | solution.py:845
  50.9 25.6 %collective-permute-start.16 = (bf16[136,1088]{1,0:T(8,128)(2,1)}, bf16[136,1088]{1,0:T(8,128)(2,1)}, u32[]{:S(2)}, u32[]{:S(2)}) collective-permute-start(bf16[136,1088]{1,0:T(8,128)(2,1)} %constant_dynamic-slice_fusion.11), channel_id=1, source_target_pairs={{0,16},{8,24},{16,0},{24,8},{1,17},{9,25},{17,1},{25,9},{2,18},{10... | collective-permute-start | bytes 887816 | tf_op jit(solution)/shard_map/ppermute | solution.py:845
  67.4 24.1 %collective-permute-start.25 = (bf16[136,1088]{1,0:T(8,128)(2,1)}, bf16[136,1088]{1,0:T(8,128)(2,1)}, u32[]{:S(2)}, u32[]{:S(2)}) collective-permute-start(bf16[136,1088]{1,0:T(8,128)(2,1)} %get-tuple-element.200), channel_id=1, source_target_pairs={{0,16},{8,24},{16,0},{24,8},{1,17},{9,25},{17,1},{25,9},{2,18},{10... | collective-permute-start | bytes 887816 | tf_op jit(solution)/shard_map/ppermute | solution.py:845
  75.3 16.5 %collective-permute-start.26 = (bf16[136,1088]{1,0:T(8,128)(2,1)S(1)}, bf16[136,1088]{1,0:T(8,128)(2,1)}, u32[]{:S(2)}, u32[]{:S(2)}) collective-permute-start(bf16[136,1088]{1,0:T(8,128)(2,1)S(1)} %copy-done.17), channel_id=1, source_target_pairs={{0,24},{8,16},{16,8},{24,0},{1,25},{9,17},{17,9},{25,1},{2,26},{10... | collective-permute-start | bytes 887816 | tf_op jit(solution)/shard_map/ppermute | solution.py:845
  78.2 18.7 %collective-permute-start.19 = (bf16[136,1088]{1,0:T(8,128)(2,1)}, bf16[136,1088]{1,0:T(8,128)(2,1)}, u32[]{:S(2)}, u32[]{:S(2)}) collective-permute-start(bf16[136,1088]{1,0:T(8,128)(2,1)} %collective-permute-done.16.refs_2_), channel_id=1, source_target_pairs={{0,1},{1,0},{2,3},{3,2},{4,5},{5,4},{6,7},{7,6},{8,9},{9,8},{10,11... | collective-permute-start | bytes 887816 | tf_op jit(solution)/shard_map/ppermute | solution.py:848
  81.1 16.7 %collective-permute-start.20 = (bf16[136,1088]{1,0:T(8,128)(2,1)}, bf16[136,1088]{1,0:T(8,128)(2,1)}, u32[]{:S(2)}, u32[]{:S(2)}) collective-permute-start(bf16[136,1088]{1,0:T(8,128)(2,1)} %collective-permute-done.17.refs_4_), channel_id=1, source_target_pairs={{0,1},{1,0},{2,3},{3,2},{4,5},{5,4},{6,7},{7,6},{8,9},{9,8},{10,11... | collective-permute-start | bytes 887816 | tf_op jit(solution)/shard_map/ppermute | solution.py:848
  97.0 16.7 %collective-permute-start.27 = (bf16[136,1088]{1,0:T(8,128)(2,1)S(1)}, bf16[136,1088]{1,0:T(8,128)(2,1)S(1)}, u32[]{:S(2)}, u32[]{:S(2)}) collective-permute-start(bf16[136,1088]{1,0:T(8,128)(2,1)S(1)} %collective-permute-done.24.refs_0_), channel_id=1, source_target_pairs={{0,1},{1,0},{2,3},{3,2},{4,5},{5,4},{6,7},{7,6},{8,9},{9,8},{10,11... | collective-permute-start | bytes 887816 | tf_op jit(solution)/shard_map/ppermute | solution.py:848
  97.8 18.2 %collective-permute-start.28 = (bf16[136,1088]{1,0:T(8,128)(2,1)}, bf16[136,1088]{1,0:T(8,128)(2,1)}, u32[]{:S(2)}, u32[]{:S(2)}) collective-permute-start(bf16[136,1088]{1,0:T(8,128)(2,1)} %collective-permute-done.25.refs_2_), channel_id=1, source_target_pairs={{0,1},{1,0},{2,3},{3,2},{4,5},{5,4},{6,7},{7,6},{8,9},{9,8},{10,11... | collective-permute-start | bytes 887816 | tf_op jit(solution)/shard_map/ppermute | solution.py:848
  113.6 28.8 %collective-permute-start.32 = (bf16[128,1088]{1,0:T(8,128)(2,1)S(1)}, bf16[128,1088]{1,0:T(8,128)(2,1)}, u32[]{:S(2)}, u32[]{:S(2)}) collective-permute-start(bf16[128,1088]{1,0:T(8,128)(2,1)S(1)} %bitcast.178), channel_id=1, source_target_pairs={{0,24},{8,16},{16,8},{24,0},{1,25},{9,17},{17,9},{25,1},{2,26},{10... | collective-permute-start | bytes 835592 | tf_op jit(solution)/shard_map/ppermute | solution.py:845
  116.1 26.4 %collective-permute-start.31 = (bf16[128,1088]{1,0:T(8,128)(2,1)S(1)}, bf16[128,1088]{1,0:T(8,128)(2,1)}, u32[]{:S(2)}, u32[]{:S(2)}) collective-permute-start(bf16[128,1088]{1,0:T(8,128)(2,1)S(1)} %bitcast.179), channel_id=1, source_target_pairs={{0,16},{8,24},{16,0},{24,8},{1,17},{9,25},{17,1},{25,9},{2,18},{10... | collective-permute-start | bytes 835592 | tf_op jit(solution)/shard_map/ppermute | solution.py:845
  116.3 26.1 %collective-permute-start.30 = (bf16[128,1088]{1,0:T(8,128)(2,1)S(1)}, bf16[128,1088]{1,0:T(8,128)(2,1)}, u32[]{:S(2)}, u32[]{:S(2)}) collective-permute-start(bf16[128,1088]{1,0:T(8,128)(2,1)S(1)} %bitcast.180), channel_id=1, source_target_pairs={{0,8},{8,0},{16,24},{24,16},{1,9},{9,1},{17,25},{25,17},{2,10},{10... | collective-permute-start | bytes 835592 | tf_op jit(solution)/shard_map/ppermute | solution.py:845
  123.8 85.5 %collective-permute-start.52 = (bf16[128,272]{1,0:T(8,128)(2,1)}, bf16[128,272]{1,0:T(8,128)(2,1)}, u32[]{:S(2)}, u32[]{:S(2)}) collective-permute-start(bf16[128,272]{1,0:T(8,128)(2,1)} %get-tuple-element.226), channel_id=1, source_target_pairs={{0,8},{8,0},{16,24},{24,16},{1,9},{9,1},{17,25},{25,17},{2,10},{10... | collective-permute-start | bytes 208904 | tf_op jit(solution)/shard_map/ppermute | solution.py:845
  135.2 74.1 %collective-permute-start.53 = (bf16[128,272]{1,0:T(8,128)(2,1)}, bf16[128,272]{1,0:T(8,128)(2,1)}, u32[]{:S(2)}, u32[]{:S(2)}) collective-permute-start(bf16[128,272]{1,0:T(8,128)(2,1)} %get-tuple-element.225), channel_id=1, source_target_pairs={{0,16},{8,24},{16,0},{24,8},{1,17},{9,25},{17,1},{25,9},{2,18},{10... | collective-permute-start | bytes 208904 | tf_op jit(solution)/shard_map/ppermute | solution.py:845
  162.1 47.2 %collective-permute-start.54 = (bf16[128,272]{1,0:T(8,128)(2,1)S(1)}, bf16[128,272]{1,0:T(8,128)(2,1)}, u32[]{:S(2)}, u32[]{:S(2)}) collective-permute-start(bf16[128,272]{1,0:T(8,128)(2,1)S(1)} %copy-done.39), channel_id=1, source_target_pairs={{0,24},{8,16},{16,8},{24,0},{1,25},{9,17},{17,9},{25,1},{2,26},{10... | collective-permute-start | bytes 208904 | tf_op jit(solution)/shard_map/ppermute | solution.py:845
  180.4 35.3 %collective-permute-start.33 = (bf16[4,136,1088]{2,1,0:T(8,128)(2,1)}, bf16[4,136,1088]{2,1,0:T(8,128)(2,1)}, u32[]{:S(2)}, u32[]{:S(2)}) collective-permute-start(bf16[4,136,1088]{2,1,0:T(8,128)(2,1)} %constant_dynamic-slice_fusion.9), channel_id=1, source_target_pairs={{0,1},{1,0},{2,3},{3,2},{4,5},{5,4},{6,7},{7,6},{8,9},{9,8},{10,11... | collective-permute-start | bytes 3551240 | tf_op jit(solution)/shard_map/ppermute | solution.py:848
  187.8 33.6 %collective-permute-start.75 = (bf16[4,136,1088]{2,1,0:T(8,128)(2,1)}, bf16[4,136,1088]{2,1,0:T(8,128)(2,1)}, u32[]{:S(2)}, u32[]{:S(2)}) collective-permute-start(bf16[4,136,1088]{2,1,0:T(8,128)(2,1)} %dynamic-slice_bitcast_fusion), channel_id=1, source_target_pairs={{0,1},{1,0},{2,3},{3,2},{4,5},{5,4},{6,7},{7,6},{8,9},{9,8},{10,11... | collective-permute-start | bytes 3551240 | tf_op jit(solution)/shard_map/ppermute | solution.py:848
  231.4 32.7 %collective-permute-start.49 = (bf16[128,1088]{1,0:T(8,128)(2,1)}, bf16[128,1088]{1,0:T(8,128)(2,1)}, u32[]{:S(2)}, u32[]{:S(2)}) collective-permute-start(bf16[128,1088]{1,0:T(8,128)(2,1)} %get-tuple-element.212), channel_id=1, source_target_pairs={{0,8},{8,0},{16,24},{24,16},{1,9},{9,1},{17,25},{25,17},{2,10},{10... | collective-permute-start | bytes 835592 | tf_op jit(solution)/shard_map/ppermute | solution.py:845
  231.6 32.5 %collective-permute-start.50 = (bf16[128,1088]{1,0:T(8,128)(2,1)}, bf16[128,1088]{1,0:T(8,128)(2,1)}, u32[]{:S(2)}, u32[]{:S(2)}) collective-permute-start(bf16[128,1088]{1,0:T(8,128)(2,1)} %get-tuple-element.211), channel_id=1, source_target_pairs={{0,16},{8,24},{16,0},{24,8},{1,17},{9,25},{17,1},{25,9},{2,18},{10... | collective-permute-start | bytes 835592 | tf_op jit(solution)/shard_map/ppermute | solution.py:845
  235.4 28.7 %collective-permute-start.51 = (bf16[128,1088]{1,0:T(8,128)(2,1)}, bf16[128,1088]{1,0:T(8,128)(2,1)}, u32[]{:S(2)}, u32[]{:S(2)}) collective-permute-start(bf16[128,1088]{1,0:T(8,128)(2,1)} %get-tuple-element.210), channel_id=1, source_target_pairs={{0,24},{8,16},{16,8},{24,0},{1,25},{9,17},{17,9},{25,1},{2,26},{10... | collective-permute-start | bytes 835592 | tf_op jit(solution)/shard_map/ppermute | solution.py:845
  235.4 24.7 %collective-permute-start.57 = (bf16[136,960]{1,0:T(8,128)(2,1)}, bf16[136,960]{1,0:T(8,128)(2,1)}, u32[]{:S(2)}, u32[]{:S(2)}) collective-permute-start(bf16[136,960]{1,0:T(8,128)(2,1)} %get-tuple-element.220), channel_id=1, source_target_pairs={{0,16},{8,24},{16,0},{24,8},{1,17},{9,25},{17,1},{25,9},{2,18},{10... | collective-permute-start | bytes 783368 | tf_op jit(solution)/shard_map/ppermute | solution.py:845
  240.5 20.9 %collective-permute-start.58 = (bf16[136,960]{1,0:T(8,128)(2,1)}, bf16[136,960]{1,0:T(8,128)(2,1)}, u32[]{:S(2)}, u32[]{:S(2)}) collective-permute-start(bf16[136,960]{1,0:T(8,128)(2,1)} %get-tuple-element.219), channel_id=1, source_target_pairs={{0,24},{8,16},{16,8},{24,0},{1,25},{9,17},{17,9},{25,1},{2,26},{10... | collective-permute-start | bytes 783368 | tf_op jit(solution)/shard_map/ppermute | solution.py:845
  261.4 36.4 %collective-permute-start.43 = (bf16[2,136,1088]{2,1,0:T(8,128)(2,1)S(1)}, bf16[2,136,1088]{2,1,0:T(8,128)(2,1)}, u32[]{:S(2)}, u32[]{:S(2)}) collective-permute-start(bf16[2,136,1088]{2,1,0:T(8,128)(2,1)S(1)} %constant_dynamic-slice_fusion.7), channel_id=1, source_target_pairs={{0,2},{1,3},{2,0},{3,1},{4,6},{5,7},{6,4},{7,5},{8,10},{9,11},{10,... | collective-permute-start | bytes 1775624 | tf_op jit(solution)/shard_map/ppermute | solution.py:848
  280.1 19.2 %collective-permute-start.77 = (bf16[136,1088]{1,0:T(8,128)(2,1)S(1)}, bf16[136,1088]{1,0:T(8,128)(2,1)S(1)}, u32[]{:S(2)}, u32[]{:S(2)}) collective-permute-start(bf16[136,1088]{1,0:T(8,128)(2,1)S(1)} %dynamic-slice_bitcast_fusion.1), channel_id=1, source_target_pairs={{0,4},{1,5},{2,6},{3,7},{4,0},{5,1},{6,2},{7,3},{8,12},{9,13},{10,... | collective-permute-start | bytes 887816 | tf_op jit(solution)/shard_map/ppermute | solution.py:848
  284.0 46.6 %collective-permute-start.59 = (bf16[2,136,1088]{2,1,0:T(8,128)(2,1)S(1)}, bf16[2,136,1088]{2,1,0:T(8,128)(2,1)S(1)}, u32[]{:S(2)}, u32[]{:S(2)}) collective-permute-start(bf16[2,136,1088]{2,1,0:T(8,128)(2,1)S(1)} %constant_dynamic-slice_fusion.5), channel_id=1, source_target_pairs={{0,2},{1,3},{2,0},{3,1},{4,6},{5,7},{6,4},{7,5},{8,10},{9,11},{10,... | collective-permute-start | bytes 1775624 | tf_op jit(solution)/shard_map/ppermute | solution.py:848
  295.6 36.8 %collective-permute-start.90 = (f32[12,272]{1,0:T(8,128)S(1)}, f32[12,272]{1,0:T(8,128)S(1)}, u32[]{:S(2)}, u32[]{:S(2)}) collective-permute-start(f32[12,272]{1,0:T(8,128)S(1)} %add.376), channel_id=1, source_target_pairs={{0,4},{1,5},{2,6},{3,7},{4,0},{5,1},{6,2},{7,3},{8,12},{9,13},{10,... | collective-permute-start | bytes 39176 | tf_op jit(solution)/shard_map/ppermute | solution.py:848
  299.1 16.2 %collective-permute-start.44 = (bf16[136,1088]{1,0:T(8,128)(2,1)S(1)}, bf16[136,1088]{1,0:T(8,128)(2,1)S(1)}, u32[]{:S(2)}, u32[]{:S(2)}) collective-permute-start(bf16[136,1088]{1,0:T(8,128)(2,1)S(1)} %dynamic-slice_bitcast_fusion.3), channel_id=1, source_target_pairs={{0,4},{1,5},{2,6},{3,7},{4,0},{5,1},{6,2},{7,3},{8,12},{9,13},{10,... | collective-permute-start | bytes 887816 | tf_op jit(solution)/shard_map/ppermute | solution.py:848
  300.1 33.1 %collective-permute-start.78 = (bf16[136,1088]{1,0:T(8,128)(2,1)}, bf16[136,1088]{1,0:T(8,128)(2,1)}, u32[]{:S(2)}, u32[]{:S(2)}) collective-permute-start(bf16[136,1088]{1,0:T(8,128)(2,1)} %fusion.16.refs_0_), channel_id=1, source_target_pairs={{0,4},{1,5},{2,6},{3,7},{4,0},{5,1},{6,2},{7,3},{8,12},{9,13},{10,... | collective-permute-start | bytes 887816 | tf_op jit(solution)/shard_map/ppermute | solution.py:848
  302.4 33.2 %collective-permute-start.79 = (bf16[136,1088]{1,0:T(8,128)(2,1)}, bf16[136,1088]{1,0:T(8,128)(2,1)}, u32[]{:S(2)}, u32[]{:S(2)}) collective-permute-start(bf16[136,1088]{1,0:T(8,128)(2,1)} %fusion.16.refs_0_), channel_id=1, source_target_pairs={{0,2},{1,3},{2,0},{3,1},{4,6},{5,7},{6,4},{7,5},{8,10},{9,11},{10,... | collective-permute-start | bytes 887816 | tf_op jit(solution)/shard_map/ppermute | solution.py:848
  315.4 20.2 %collective-permute-start.81 = (bf16[136,1088]{1,0:T(8,128)(2,1)}, bf16[136,1088]{1,0:T(8,128)(2,1)}, u32[]{:S(2)}, u32[]{:S(2)}) collective-permute-start(bf16[136,1088]{1,0:T(8,128)(2,1)} %fusion.16.refs_0_), channel_id=1, source_target_pairs={{0,1},{1,0},{2,3},{3,2},{4,5},{5,4},{6,7},{7,6},{8,9},{9,8},{10,11... | collective-permute-start | bytes 887816 | tf_op jit(solution)/shard_map/ppermute | solution.py:848
  331.5 22.8 %collective-permute-start.60 = (bf16[136,1088]{1,0:T(8,128)(2,1)}, bf16[136,1088]{1,0:T(8,128)(2,1)}, u32[]{:S(2)}, u32[]{:S(2)}) collective-permute-start(bf16[136,1088]{1,0:T(8,128)(2,1)} %dynamic-slice_bitcast_fusion.2), channel_id=1, source_target_pairs={{0,4},{1,5},{2,6},{3,7},{4,0},{5,1},{6,2},{7,3},{8,12},{9,13},{10,... | collective-permute-start | bytes 887816 | tf_op jit(solution)/shard_map/ppermute | solution.py:848
  333.2 30.7 %collective-permute-start.68 = (bf16[136,1088]{1,0:T(8,128)(2,1)}, bf16[136,1088]{1,0:T(8,128)(2,1)}, u32[]{:S(2)}, u32[]{:S(2)}) collective-permute-start(bf16[136,1088]{1,0:T(8,128)(2,1)} %fusion.18.refs_0_), channel_id=1, source_target_pairs={{0,4},{1,5},{2,6},{3,7},{4,0},{5,1},{6,2},{7,3},{8,12},{9,13},{10,... | collective-permute-start | bytes 887816 | tf_op jit(solution)/shard_map/ppermute | solution.py:848
  335.6 28.4 %collective-permute-start.69 = (bf16[136,1088]{1,0:T(8,128)(2,1)}, bf16[136,1088]{1,0:T(8,128)(2,1)}, u32[]{:S(2)}, u32[]{:S(2)}) collective-permute-start(bf16[136,1088]{1,0:T(8,128)(2,1)} %fusion.18.refs_0_), channel_id=1, source_target_pairs={{0,2},{1,3},{2,0},{3,1},{4,6},{5,7},{6,4},{7,5},{8,10},{9,11},{10,... | collective-permute-start | bytes 887816 | tf_op jit(solution)/shard_map/ppermute | solution.py:848
  335.6 28.4 %collective-permute-start.71 = (bf16[136,1088]{1,0:T(8,128)(2,1)}, bf16[136,1088]{1,0:T(8,128)(2,1)S(1)}, u32[]{:S(2)}, u32[]{:S(2)}) collective-permute-start(bf16[136,1088]{1,0:T(8,128)(2,1)} %fusion.18.refs_0_), channel_id=1, source_target_pairs={{0,1},{1,0},{2,3},{3,2},{4,5},{5,4},{6,7},{7,6},{8,9},{9,8},{10,11... | collective-permute-start | bytes 887816 | tf_op jit(solution)/shard_map/ppermute | solution.py:848
  364.0 16.8 %collective-permute-start.70 = (bf16[136,1088]{1,0:T(8,128)(2,1)}, bf16[136,1088]{1,0:T(8,128)(2,1)S(1)}, u32[]{:S(2)}, u32[]{:S(2)}) collective-permute-start(bf16[136,1088]{1,0:T(8,128)(2,1)} %collective-permute-done.68.refs_1_), channel_id=1, source_target_pairs={{0,2},{1,3},{2,0},{3,1},{4,6},{5,7},{6,4},{7,5},{8,10},{9,11},{10,... | collective-permute-start | bytes 887816 | tf_op jit(solution)/shard_map/ppermute | solution.py:848
  364.0 16.7 %collective-permute-start.61 = (bf16[136,1088]{1,0:T(8,128)(2,1)}, bf16[136,1088]{1,0:T(8,128)(2,1)}, u32[]{:S(2)}, u32[]{:S(2)}) collective-permute-start(bf16[136,1088]{1,0:T(8,128)(2,1)} %fusion.17.refs_0_), channel_id=1, source_target_pairs={{0,4},{1,5},{2,6},{3,7},{4,0},{5,1},{6,2},{7,3},{8,12},{9,13},{10,... | collective-permute-start | bytes 887816 | tf_op jit(solution)/shard_map/ppermute | solution.py:848
  367.6 18.5 %collective-permute-start.72 = (bf16[136,1088]{1,0:T(8,128)(2,1)}, bf16[136,1088]{1,0:T(8,128)(2,1)}, u32[]{:S(2)}, u32[]{:S(2)}) collective-permute-start(bf16[136,1088]{1,0:T(8,128)(2,1)} %collective-permute-done.68.refs_1_), channel_id=1, source_target_pairs={{0,1},{1,0},{2,3},{3,2},{4,5},{5,4},{6,7},{7,6},{8,9},{9,8},{10,11... | collective-permute-start | bytes 887816 | tf_op jit(solution)/shard_map/ppermute | solution.py:848
  368.2 18.9 %collective-permute-start.73 = (bf16[136,1088]{1,0:T(8,128)(2,1)}, bf16[136,1088]{1,0:T(8,128)(2,1)}, u32[]{:S(2)}, u32[]{:S(2)}) collective-permute-start(bf16[136,1088]{1,0:T(8,128)(2,1)} %collective-permute-done.69.refs_2_), channel_id=1, source_target_pairs={{0,1},{1,0},{2,3},{3,2},{4,5},{5,4},{6,7},{7,6},{8,9},{9,8},{10,11... | collective-permute-start | bytes 887816 | tf_op jit(solution)/shard_map/ppermute | solution.py:848
  368.3 18.9 %collective-permute-start.84 = (bf16[136,1088]{1,0:T(8,128)(2,1)}, bf16[136,1088]{1,0:T(8,128)(2,1)}, u32[]{:S(2)}, u32[]{:S(2)}) collective-permute-start(bf16[136,1088]{1,0:T(8,128)(2,1)} %collective-permute-done.80.refs_3_), channel_id=1, source_target_pairs={{0,1},{1,0},{2,3},{3,2},{4,5},{5,4},{6,7},{7,6},{8,9},{9,8},{10,11... | collective-permute-start | bytes 887816 | tf_op jit(solution)/shard_map/ppermute | solution.py:848
  386.1 23.6 %collective-permute-start.64 = (bf16[136,1088]{1,0:T(8,128)(2,1)}, bf16[136,1088]{1,0:T(8,128)(2,1)S(1)}, u32[]{:S(2)}, u32[]{:S(2)}) collective-permute-start(bf16[136,1088]{1,0:T(8,128)(2,1)} %fusion.17.refs_0_), channel_id=1, source_target_pairs={{0,1},{1,0},{2,3},{3,2},{4,5},{5,4},{6,7},{7,6},{8,9},{9,8},{10,11... | collective-permute-start | bytes 887816 | tf_op jit(solution)/shard_map/ppermute | solution.py:848
  387.2 17.3 %collective-permute-start.74 = (bf16[136,1088]{1,0:T(8,128)(2,1)}, bf16[136,1088]{1,0:T(8,128)(2,1)S(1)}, u32[]{:S(2)}, u32[]{:S(2)}) collective-permute-start(bf16[136,1088]{1,0:T(8,128)(2,1)} %copy-done.15), channel_id=1, source_target_pairs={{0,1},{1,0},{2,3},{3,2},{4,5},{5,4},{6,7},{7,6},{8,9},{9,8},{10,11... | collective-permute-start | bytes 887816 | tf_op jit(solution)/shard_map/ppermute | solution.py:848
  387.2 22.5 %collective-permute-start.65 = (bf16[136,1088]{1,0:T(8,128)(2,1)}, bf16[136,1088]{1,0:T(8,128)(2,1)}, u32[]{:S(2)}, u32[]{:S(2)}) collective-permute-start(bf16[136,1088]{1,0:T(8,128)(2,1)} %collective-permute-done.61.refs_1_), channel_id=1, source_target_pairs={{0,1},{1,0},{2,3},{3,2},{4,5},{5,4},{6,7},{7,6},{8,9},{9,8},{10,11... | collective-permute-start | bytes 887816 | tf_op jit(solution)/shard_map/ppermute | solution.py:848
  389.6 20.2 %collective-permute-start.66 = (bf16[136,1088]{1,0:T(8,128)(2,1)}, bf16[136,1088]{1,0:T(8,128)(2,1)}, u32[]{:S(2)}, u32[]{:S(2)}) collective-permute-start(bf16[136,1088]{1,0:T(8,128)(2,1)} %collective-permute-done.62.refs_2_), channel_id=1, source_target_pairs={{0,1},{1,0},{2,3},{3,2},{4,5},{5,4},{6,7},{7,6},{8,9},{9,8},{10,11... | collective-permute-start | bytes 887816 | tf_op jit(solution)/shard_map/ppermute | solution.py:848
  (101 other events, 1320.2 us)
where the time goes:
time: 423 us; the launch traced here: 415 us
  waiting for transfers between devices  126 us (30%)
  starting transfers between devices  104 us (25%)
  Pallas kernels  62 us (15%)
  local copies, waits for them, and re-layouts  57.1 us (13%)
  matrix products  32.7 us (8%)
  other arithmetic  31.5 us (7%)
    ppermute x48, waiting for transfers between devices, send(): return lax.ppermute(value, 'shard', [(j, j ^ k) for j in range(count)])  65.4 us
    ppermute x43, starting transfers between devices, cross(): return lax.ppermute(value, 'dp', [(j, j ^ k) for j in range(8)])  64.6 us
    ppermute x43, waiting for transfers between devices, cross(): return lax.ppermute(value, 'dp', [(j, j ^ k) for j in range(8)])  60.4 us
    ppermute x48, starting transfers between devices, send(): return lax.ppermute(value, 'shard', [(j, j ^ k) for j in range(count)])  39.5 us
    pallas_call x3, Pallas kernels, unfold(): call(kernel, [jax.ShapeDtypeStruct(shape, F32) for shape in shapes], [pl....  13.1 us
    unnamed x131, local copies, waits for them, and re-layouts  13 us
    dot_general x3, matrix products, matmul(): return jnp.dot(left_side, right_side, preferred_element_type=F32)  13 us
    convert_element_type x10, other arithmetic, added(): return (left.astype(F32) + right.astype(F32)).astype(BF16)  12.9 us
  transfers between devices with their start and end apart: 91, of which 21 were waited for; matrix products, arithmetic and copies ran while one was open for 27% of the time, Pallas kernels for 14%

commit v1 on v0

--- a/solution.py
+++ b/solution.py
@@ -974,7 +974,7 @@
         qkv, grad_attended, grad_last, attended, last, logs, rows_info, cols_info, heads
     )
     up_pieces = list(lax.optimization_barrier((*up_pieces, head_sums)))[:-1]
-    (up_weight_grad,), up_one = reduce_far(assemble(up_pieces, slots, count), "columns")
+    (up_weight_grad,), _ = reduce_far(assemble(up_pieces, slots, count), "columns")
     qkv_keep, qkv_give = grad_columns(first_in, grad_qkv, core, count)
     qkv_part = added(qkv_keep, cross(qkv_give, 1))
     late_qkv, _ = lax.optimization_barrier((grad_qkv, qkv_part))
@@ -993,9 +993,6 @@
     first_hat, first_inv = normalise(residual_in)
     input_grad = grad_middle + norm_backward(grad_first, first_hat, first_inv, first_gain_full)
     square, _ = reduce_far(placed, "arrays")
-    late_activated, _ = lax.optimization_barrier((activated, up_one))
-    output_rows = matmul(late_activated, down_weight)
-    outputs = (middle + scatter_sum(output_rows) + vectors[3]).astype(BF16)
 
     def to_full(row):
         main = lax.dynamic_update_slice(
@@ -1021,7 +1018,13 @@
         mine = mine + send(pick(rows, slots[k]), k)
     summed = jnp.concatenate([mine, up_bias_part.reshape(count, own)], axis=0)
     for k in (1, 2, 4):
-        summed = summed + cross(summed, k)
+        given = cross(summed, k)
+        summed = summed + given
+        if k == 2:
+            third = given
+    late_activated, _ = lax.optimization_barrier((activated, third))
+    output_rows = matmul(late_activated, down_weight)
+    outputs = (middle + scatter_sum(output_rows) + vectors[3]).astype(BF16)
     return (
         outputs[None],
         input_grad[None],

time: 423 us -> 434 us (1.026)
  the two profiles are of different devices: /device:TPU:5 before, /device:TPU:29 now
where the time goes in v1:
time: 434 us; the launch traced here: 426 us
  waiting for transfers between devices  159 us (37%)
  starting transfers between devices  84.7 us (20%)
  Pallas kernels  61.9 us (14%)
  local copies, waits for them, and re-layouts  58.8 us (14%)
  matrix products  31.3 us (7%)
  other arithmetic  27.8 us (6%)
    ppermute x43, waiting for transfers between devices, cross(): return lax.ppermute(value, 'dp', [(j, j ^ k) for j in range(8)])  105 us
    ppermute x48, waiting for transfers between devices, send(): return lax.ppermute(value, 'shard', [(j, j ^ k) for j in range(count)])  54.5 us
    ppermute x43, starting transfers between devices, cross(): return lax.ppermute(value, 'dp', [(j, j ^ k) for j in range(8)])  43 us
    ppermute x48, starting transfers between devices, send(): return lax.ppermute(value, 'shard', [(j, j ^ k) for j in range(count)])  41.6 us
    unnamed x149, local copies, waits for them, and re-layouts  15.1 us
    pallas_call x3, Pallas kernels, unfold(): call(kernel, [jax.ShapeDtypeStruct(shape, F32) for shape in shapes], [pl....  13.1 us
    dot_general x3, matrix products, matmul(): return jnp.dot(left_side, right_side, preferred_element_type=F32)  12.9 us
    pallas_call x4, Pallas kernels, assemble(): call(kernel, jax.ShapeDtypeStruct((total,) + shape, pieces[0].dtype), pl....  12.1 us
  transfers between devices with their start and end apart: 91, of which 24 were waited for; matrix products, arithmetic and copies ran while one was open for 25% of the time, Pallas kernels for 14%

profile of v1, /device:TPU:29, one launch (start us, length us, event | category | flops | bytes accessed | tf_op | source)
XLA Modules:
  0.0 425.8 jit_solution(10198271918065255329)
XLA Ops:
  14.6 3.8 slice_bitcast_fusion.3
  29.0 2.7 shard_map.305
  35.5 9.4 %collective-permute-done.6.refs_0_ = bf16[136,960]{1,0:T(8,128)(2,1)} collective-permute-done((bf16[136,960]{1,0:T(8,128)(2,1)}, bf16[136,960]{1,0:T(8,128)(2,1)}, u32[]{:S(2)}, u32[]{:S(2)}) %collective-permute-start.6) | collective-permute-done | bytes 261152 | tf_op jit(solution)/shard_map/ppermute | solution.py:845
  48.0 3.5 collective-permute-done.10.refs_4_
  51.7 7.4 %collective-permute-start.7 = (bf16[136,960]{1,0:T(8,128)(2,1)}, bf16[136,960]{1,0:T(8,128)(2,1)S(1)}, u32[]{:S(2)}, u32[]{:S(2)}) collective-permute-start(bf16[136,960]{1,0:T(8,128)(2,1)} %collective-permute-done.6.refs_0_), channel_id=1, source_target_pairs={{0,1},{1,0},{2,3},{3,2},{4,5},{5,4},{6,7},{7,6},{8,9},{9,8},{10,11... | collective-permute-start | bytes 783368 | tf_op jit(solution)/shard_map/ppermute | solution.py:848
  68.2 3.1 shard_map.306
  71.3 4.6 %add_convert_fusion.2.q_ref.kv_ref = bf16[512,960]{1,0:T(8,128)(2,1)} fusion(bf16[512,1088]{1,0:T(8,128)(2,1)} %fusion.6.in_ref, bf16[1088,960]{1,0:T(8,128)(2,1)} %bitcast.174, f32[960]{0:T(1024)S(1)} %concatenate.26), kind=kOutput, calls=%fused_computation.27 | convolution fusion | flops 1070530560 | bytes 4189952 | tf_op jit(solution)/shard_map/dot_general | solution.py:40
  78.9 2.8 collective-permute-done.24.refs_0_
  83.9 8.2 %shard_map.307 = (bf16[512,256]{1,0:T(8,128)(2,1)}, bf16[128,64]{1,0:T(8,128)(2,1)}, f32[512,128]{1,0:T(8,128)}, bf16[128,256]{1,0:T(8,128)(2,1)}, bf16[128,256]{1,0:T(8,128)(2,1)}, /*index=5*/bf16[128,256]{1,0:T(8,128)(2,1)}) custom-call(bf16[512,960]{1,0:T(8,128)(2,1)} %add_convert_fusion.2.q_ref.kv_ref, bf16[512,960]{1,0:T(8,128)(2,1)} %add_convert_fusion.2.q_ref.kv_ref, ...), custom_call_target="tpu_custom_call" | custom-call | tf_op jit(solution)/shard_map/pallas_call | solution.py:659
  99.2 3.3 shard_map.308
  103.7 3.6 shard_map.309
  117.8 3.3 shard_map.310
  127.1 9.6 %collective-permute-done.23 = bf16[128,1088]{1,0:T(8,128)(2,1)S(1)} collective-permute-done((bf16[128,1088]{1,0:T(8,128)(2,1)S(1)}, bf16[128,1088]{1,0:T(8,128)(2,1)S(1)}, u32[]{:S(2)}, u32[]{:S(2)}) %collective-permute-start.23) | collective-permute-done | bytes 278560 | tf_op jit(solution)/shard_map/ppermute | solution.py:845
  138.7 5.1 %multiply_convert_fusion = (bf16[512,1088]{0,1:T(8,128)(2,1)}, f32[512,1088]{0,1:T(8,128)S(1)}) fusion(f32[1088]{0:T(1024)S(1)} %copy-done.57, bf16[512,1088]{1,0:T(8,128)(2,1)} %constant_dynamic-update-slice_fusion, bf16[1088,1088]{1,0:T(8,128)(2,1)} %bitcast.168), kind=kOutput, calls=%fused_computation.25 | convolution fusion | flops 1215496192 | bytes 6828288 | tf_op jit(solution)/shard_map/dot_general | solution.py:40
  143.8 3.7 fusion.58
  147.4 3.7 fusion.57
  151.2 3.2 convolution_convert_fusion.1
  160.9 2.8 convolution_convert_fusion
  167.7 3.3 shard_map.311
  179.0 4.0 collective-permute-done.37.refs_2_
  183.0 6.3 %collective-permute-start.67 = (bf16[4,136,1088]{2,1,0:T(8,128)(2,1)}, bf16[4,136,1088]{2,1,0:T(8,128)(2,1)}, u32[]{:S(2)}, u32[]{:S(2)}) collective-permute-start(bf16[4,136,1088]{2,1,0:T(8,128)(2,1)} %constant_dynamic-slice_fusion.2), channel_id=1, source_target_pairs={{0,1},{1,0},{2,3},{3,2},{4,5},{5,4},{6,7},{7,6},{8,9},{9,8},{10,11... | collective-permute-start | bytes 3551240 | tf_op jit(solution)/shard_map/ppermute | solution.py:848
  190.0 3.0 shard_map.312
  192.9 9.0 %shard_map.313 = (bf16[512,960]{1,0:T(8,128)(2,1)}, f32[8,320]{1,0:T(8,128)}) custom-call(bf16[512,960]{1,0:T(8,128)(2,1)} %add_convert_fusion.2.q_ref.kv_ref, bf16[512,960]{1,0:T(8,128)(2,1)} %add_convert_fusion.2.q_ref.kv_ref, bf16[512,256]{1,0:T(8,128)(2,1)} %get-tuple-element.84.grad_ref, bf16[128,64]{1,0:T(8,128)(2,1)} %get-tuple-element.85.glast_ref, ...), custom_call_target="tpu_custom_call" | custom-call | tf_op jit(solution)/shard_map/pallas_call | solution.py:780
  203.4 4.5 %shard_map.314 = (bf16[4,136,960]{2,1,0:T(8,128)(2,1)}, bf16[4,136,960]{2,1,0:T(8,128)(2,1)}) custom-call(s32[1]{0:T(128)} %bitcast.19.core_ref, bf16[512,1088]{1,0:T(8,128)(2,1)} %fusion.6.in_ref, bf16[512,960]{1,0:T(8,128)(2,1)} %get-tuple-element.92.grad_ref), custom_call_target="tpu_custom_call" | custom-call | tf_op jit(solution)/shard_map/pallas_call | solution.py:436
  216.5 2.7 collective-permute-start.68
  225.1 3.0 fusion.59
  230.9 3.2 collective-permute-done.69.refs_2_
  234.5 4.9 %collective-permute-done.47.refs_2_ = bf16[136,960]{1,0:T(8,128)(2,1)S(1)} collective-permute-done((bf16[136,960]{1,0:T(8,128)(2,1)S(1)}, bf16[136,960]{1,0:T(8,128)(2,1)S(1)}, u32[]{:S(2)}, u32[]{:S(2)}) %collective-permute-start.47) | collective-permute-done | bytes 261152 | tf_op jit(solution)/shard_map/ppermute | solution.py:845
  244.2 14.7 %collective-permute-done.48.refs_3_ = bf16[136,960]{1,0:T(8,128)(2,1)} collective-permute-done((bf16[136,960]{1,0:T(8,128)(2,1)}, bf16[136,960]{1,0:T(8,128)(2,1)}, u32[]{:S(2)}, u32[]{:S(2)}) %collective-permute-start.48) | collective-permute-done | bytes 261152 | tf_op jit(solution)/shard_map/ppermute | solution.py:845
  263.0 2.9 fusion.20
  268.9 4.5 %collective-permute-done.81 = bf16[2,136,1088]{2,1,0:T(8,128)(2,1)} collective-permute-done((bf16[2,136,1088]{2,1,0:T(8,128)(2,1)}, bf16[2,136,1088]{2,1,0:T(8,128)(2,1)}, u32[]{:S(2)}, u32[]{:S(2)}) %collective-permute-start.81) | collective-permute-done | bytes 591904 | tf_op jit(solution)/shard_map/ppermute | solution.py:848
  274.9 4.4 %collective-permute-start.53 = (f32[12,272]{1,0:T(8,128)S(1)}, f32[12,272]{1,0:T(8,128)S(1)}, u32[]{:S(2)}, u32[]{:S(2)}) collective-permute-start(f32[12,272]{1,0:T(8,128)S(1)} %pad_maximum_fusion.7), channel_id=1, source_target_pairs={{0,1},{1,0},{2,3},{3,2},{4,5},{5,4},{6,7},{7,6},{8,9},{9,8},{10,11... | collective-permute-start | bytes 39176 | tf_op jit(solution)/shard_map/ppermute | solution.py:848
  281.7 11.2 %collective-permute-done.54 = f32[12,272]{1,0:T(8,128)S(1)} collective-permute-done((f32[12,272]{1,0:T(8,128)S(1)}, f32[12,272]{1,0:T(8,128)S(1)}, u32[]{:S(2)}, u32[]{:S(2)}) %collective-permute-start.54) | collective-permute-done | bytes 13088 | tf_op jit(solution)/shard_map/ppermute | solution.py:848
  292.9 3.3 fusion.60
  301.7 5.9 %collective-permute-done.58 = bf16[2,136,1088]{2,1,0:T(8,128)(2,1)S(1)} collective-permute-done((bf16[2,136,1088]{2,1,0:T(8,128)(2,1)S(1)}, bf16[2,136,1088]{2,1,0:T(8,128)(2,1)S(1)}, u32[]{:S(2)}, u32[]{:S(2)}) %collective-permute-start.58) | collective-permute-done | bytes 591904 | tf_op jit(solution)/shard_map/ppermute | solution.py:848
  310.3 27.5 %collective-permute-done.72 = bf16[136,1088]{1,0:T(8,128)(2,1)S(1)} collective-permute-done((bf16[136,1088]{1,0:T(8,128)(2,1)S(1)}, bf16[136,1088]{1,0:T(8,128)(2,1)S(1)}, u32[]{:S(2)}, u32[]{:S(2)}) %collective-permute-start.72) | collective-permute-done | bytes 295968 | tf_op jit(solution)/shard_map/ppermute | solution.py:848
  338.8 2.6 collective-permute-start.73
  341.5 3.0 collective-permute-done.83.refs_1_
  344.5 13.4 %collective-permute-done.59 = bf16[136,1088]{1,0:T(8,128)(2,1)S(1)} collective-permute-done((bf16[136,1088]{1,0:T(8,128)(2,1)S(1)}, bf16[136,1088]{1,0:T(8,128)(2,1)S(1)}, u32[]{:S(2)}, u32[]{:S(2)}) %collective-permute-start.59) | collective-permute-done | bytes 295968 | tf_op jit(solution)/shard_map/ppermute | solution.py:848
  359.7 5.1 %collective-permute-done.73.refs_1_ = bf16[136,1088]{1,0:T(8,128)(2,1)} collective-permute-done((bf16[136,1088]{1,0:T(8,128)(2,1)S(1)}, bf16[136,1088]{1,0:T(8,128)(2,1)}, u32[]{:S(2)}, u32[]{:S(2)}) %collective-permute-start.73) | collective-permute-done | bytes 295968 | tf_op jit(solution)/shard_map/ppermute | solution.py:848
  365.5 6.1 %collective-permute-done.74.refs_2_ = bf16[136,1088]{1,0:T(8,128)(2,1)} collective-permute-done((bf16[136,1088]{1,0:T(8,128)(2,1)S(1)}, bf16[136,1088]{1,0:T(8,128)(2,1)}, u32[]{:S(2)}, u32[]{:S(2)}) %collective-permute-start.74) | collective-permute-done | bytes 295968 | tf_op jit(solution)/shard_map/ppermute | solution.py:848
  371.7 7.8 %collective-permute-done.85.refs_3_ = bf16[136,1088]{1,0:T(8,128)(2,1)} collective-permute-done((bf16[136,1088]{1,0:T(8,128)(2,1)S(1)}, bf16[136,1088]{1,0:T(8,128)(2,1)}, u32[]{:S(2)}, u32[]{:S(2)}) %collective-permute-start.85) | collective-permute-done | bytes 295968 | tf_op jit(solution)/shard_map/ppermute | solution.py:848
  380.5 11.0 %collective-permute-done.75.refs_3_ = bf16[136,1088]{1,0:T(8,128)(2,1)S(1)} collective-permute-done((bf16[136,1088]{1,0:T(8,128)(2,1)}, bf16[136,1088]{1,0:T(8,128)(2,1)S(1)}, u32[]{:S(2)}, u32[]{:S(2)}) %collective-permute-start.75) | collective-permute-done | bytes 295968 | tf_op jit(solution)/shard_map/ppermute | solution.py:848
  397.4 2.9 collective-permute-done.61.refs_2_
  402.7 4.4 %collective-permute-done.62.refs_3_ = bf16[136,1088]{1,0:T(8,128)(2,1)} collective-permute-done((bf16[136,1088]{1,0:T(8,128)(2,1)}, bf16[136,1088]{1,0:T(8,128)(2,1)}, u32[]{:S(2)}, u32[]{:S(2)}) %collective-permute-start.62) | collective-permute-done | bytes 295968 | tf_op jit(solution)/shard_map/ppermute | solution.py:848
  411.0 4.3 shard_map.319
  416.0 4.6 %shard_map.318 = f32[272,4352]{1,0:T(8,128)} custom-call(s32[3]{0:T(128)} %pad_add_fusion.4.bits_ref, bf16[136,1088]{1,0:T(8,128)(2,1)} %copy-done.11, bf16[136,1088]{1,0:T(8,128)(2,1)} %collective-permute-done.73.refs_1_, bf16[136,1088]{1,0:T(8,128)(2,1)} %collective-permute-done.74.refs_2_, bf16[136,1088]{1,0:T(8,128)(2,1)} %copy-done.20, ...), custom_call_target="tpu_custom_call" | custom-call | tf_op jit(solution)/shard_map/pallas_call | solution.py:473
  421.3 4.3 %shard_map.316 = (f32[272,1088]{1,0:T(8,128)}, f32[272,1088]{1,0:T(8,128)}, f32[272,1088]{1,0:T(8,128)}, f32[272,1088]{1,0:T(8,128)}) custom-call(s32[3]{0:T(128)} %pad_add_fusion.4.bits_ref, bf16[136,1088]{1,0:T(8,128)(2,1)} %fusion.18.refs_0_, bf16[136,1088]{1,0:T(8,128)(2,1)} %collective-permute-done.60.refs_1_, ...), custom_call_target="tpu_custom_call" | custom-call | tf_op jit(solution)/shard_map/pallas_call | solution.py:473
  (427 shorter events, 152.4 us)
Async XLA Ops:
  6.3 26.0 %collective-permute-start.5 = (bf16[8,272]{1,0:T(8,128)(2,1)S(1)}, bf16[8,272]{1,0:T(8,128)(2,1)S(1)}, u32[]{:S(2)}, u32[]{:S(2)}) collective-permute-start(bf16[8,272]{1,0:T(8,128)(2,1)S(1)} %stack.209), channel_id=1, source_target_pairs={{0,24},{8,16},{16,8},{24,0},{1,25},{9,17},{17,9},{25,1},{2,26},{10... | collective-permute-start | bytes 13064 | tf_op jit(solution)/shard_map/ppermute | solution.py:845
  7.5 25.1 %collective-permute-start.4 = (bf16[8,272]{1,0:T(8,128)(2,1)S(1)}, bf16[8,272]{1,0:T(8,128)(2,1)S(1)}, u32[]{:S(2)}, u32[]{:S(2)}) collective-permute-start(bf16[8,272]{1,0:T(8,128)(2,1)S(1)} %stack.209), channel_id=1, source_target_pairs={{0,16},{8,24},{16,0},{24,8},{1,17},{9,25},{17,1},{25,9},{2,18},{10... | collective-permute-start | bytes 13064 | tf_op jit(solution)/shard_map/ppermute | solution.py:845
  8.8 25.0 %collective-permute-start.3 = (bf16[8,272]{1,0:T(8,128)(2,1)S(1)}, bf16[8,272]{1,0:T(8,128)(2,1)S(1)}, u32[]{:S(2)}, u32[]{:S(2)}) collective-permute-start(bf16[8,272]{1,0:T(8,128)(2,1)S(1)} %stack.209), channel_id=1, source_target_pairs={{0,8},{8,0},{16,24},{24,16},{1,9},{9,1},{17,25},{25,17},{2,10},{10... | collective-permute-start | bytes 13064 | tf_op jit(solution)/shard_map/ppermute | solution.py:845
  10.2 41.5 %collective-permute-start.2 = (bf16[128,1088]{1,0:T(8,128)(2,1)S(1)}, bf16[128,1088]{1,0:T(8,128)(2,1)S(1)}, u32[]{:S(2)}, u32[]{:S(2)}) collective-permute-start(bf16[128,1088]{1,0:T(8,128)(2,1)S(1)} %bitcast.156), channel_id=1, source_target_pairs={{0,24},{8,16},{16,8},{24,0},{1,25},{9,17},{17,9},{25,1},{2,26},{10... | collective-permute-start | bytes 835592 | tf_op jit(solution)/shard_map/ppermute | solution.py:845
  11.4 47.7 %collective-permute-start.1 = (bf16[128,1088]{1,0:T(8,128)(2,1)S(1)}, bf16[128,1088]{1,0:T(8,128)(2,1)S(1)}, u32[]{:S(2)}, u32[]{:S(2)}) collective-permute-start(bf16[128,1088]{1,0:T(8,128)(2,1)S(1)} %bitcast.157), channel_id=1, source_target_pairs={{0,16},{8,24},{16,0},{24,8},{1,17},{9,25},{17,1},{25,9},{2,18},{10... | collective-permute-start | bytes 835592 | tf_op jit(solution)/shard_map/ppermute | solution.py:845
  32.3 26.9 %collective-permute-start = (bf16[128,1088]{1,0:T(8,128)(2,1)S(1)}, bf16[128,1088]{1,0:T(8,128)(2,1)}, u32[]{:S(2)}, u32[]{:S(2)}) collective-permute-start(bf16[128,1088]{1,0:T(8,128)(2,1)S(1)} %bitcast.158), channel_id=1, source_target_pairs={{0,8},{8,0},{16,24},{24,16},{1,9},{9,1},{17,25},{25,17},{2,10},{10... | collective-permute-start | bytes 835592 | tf_op jit(solution)/shard_map/ppermute | solution.py:845
  46.8 29.1 %collective-permute-start.15 = (bf16[136,1088]{1,0:T(8,128)(2,1)}, bf16[136,1088]{1,0:T(8,128)(2,1)}, u32[]{:S(2)}, u32[]{:S(2)}) collective-permute-start(bf16[136,1088]{1,0:T(8,128)(2,1)} %constant_dynamic-slice_fusion.11), channel_id=1, source_target_pairs={{0,8},{8,0},{16,24},{24,16},{1,9},{9,1},{17,25},{25,17},{2,10},{10... | collective-permute-start | bytes 887816 | tf_op jit(solution)/shard_map/ppermute | solution.py:845
  51.5 25.7 %collective-permute-start.16 = (bf16[136,1088]{1,0:T(8,128)(2,1)}, bf16[136,1088]{1,0:T(8,128)(2,1)}, u32[]{:S(2)}, u32[]{:S(2)}) collective-permute-start(bf16[136,1088]{1,0:T(8,128)(2,1)} %constant_dynamic-slice_fusion.11), channel_id=1, source_target_pairs={{0,16},{8,24},{16,0},{24,8},{1,17},{9,25},{17,1},{25,9},{2,18},{10... | collective-permute-start | bytes 887816 | tf_op jit(solution)/shard_map/ppermute | solution.py:845
  67.9 24.1 %collective-permute-start.25 = (bf16[136,1088]{1,0:T(8,128)(2,1)}, bf16[136,1088]{1,0:T(8,128)(2,1)}, u32[]{:S(2)}, u32[]{:S(2)}) collective-permute-start(bf16[136,1088]{1,0:T(8,128)(2,1)} %get-tuple-element.200), channel_id=1, source_target_pairs={{0,16},{8,24},{16,0},{24,8},{1,17},{9,25},{17,1},{25,9},{2,18},{10... | collective-permute-start | bytes 887816 | tf_op jit(solution)/shard_map/ppermute | solution.py:845
  78.9 19.4 %collective-permute-start.19 = (bf16[136,1088]{1,0:T(8,128)(2,1)}, bf16[136,1088]{1,0:T(8,128)(2,1)}, u32[]{:S(2)}, u32[]{:S(2)}) collective-permute-start(bf16[136,1088]{1,0:T(8,128)(2,1)} %collective-permute-done.16.refs_2_), channel_id=1, source_target_pairs={{0,1},{1,0},{2,3},{3,2},{4,5},{5,4},{6,7},{7,6},{8,9},{9,8},{10,11... | collective-permute-start | bytes 887816 | tf_op jit(solution)/shard_map/ppermute | solution.py:848
  81.7 17.4 %collective-permute-start.20 = (bf16[136,1088]{1,0:T(8,128)(2,1)}, bf16[136,1088]{1,0:T(8,128)(2,1)}, u32[]{:S(2)}, u32[]{:S(2)}) collective-permute-start(bf16[136,1088]{1,0:T(8,128)(2,1)} %collective-permute-done.17.refs_4_), channel_id=1, source_target_pairs={{0,1},{1,0},{2,3},{3,2},{4,5},{5,4},{6,7},{7,6},{8,9},{9,8},{10,11... | collective-permute-start | bytes 887816 | tf_op jit(solution)/shard_map/ppermute | solution.py:848
  99.1 18.2 %collective-permute-start.28 = (bf16[136,1088]{1,0:T(8,128)(2,1)}, bf16[136,1088]{1,0:T(8,128)(2,1)}, u32[]{:S(2)}, u32[]{:S(2)}) collective-permute-start(bf16[136,1088]{1,0:T(8,128)(2,1)} %collective-permute-done.25.refs_2_), channel_id=1, source_target_pairs={{0,1},{1,0},{2,3},{3,2},{4,5},{5,4},{6,7},{7,6},{8,9},{9,8},{10,11... | collective-permute-start | bytes 887816 | tf_op jit(solution)/shard_map/ppermute | solution.py:848
  115.1 28.6 %collective-permute-start.32 = (bf16[128,1088]{1,0:T(8,128)(2,1)S(1)}, bf16[128,1088]{1,0:T(8,128)(2,1)}, u32[]{:S(2)}, u32[]{:S(2)}) collective-permute-start(bf16[128,1088]{1,0:T(8,128)(2,1)S(1)} %bitcast.178), channel_id=1, source_target_pairs={{0,24},{8,16},{16,8},{24,0},{1,25},{9,17},{17,9},{25,1},{2,26},{10... | collective-permute-start | bytes 835592 | tf_op jit(solution)/shard_map/ppermute | solution.py:845
  117.3 26.4 %collective-permute-start.31 = (bf16[128,1088]{1,0:T(8,128)(2,1)S(1)}, bf16[128,1088]{1,0:T(8,128)(2,1)}, u32[]{:S(2)}, u32[]{:S(2)}) collective-permute-start(bf16[128,1088]{1,0:T(8,128)(2,1)S(1)} %bitcast.179), channel_id=1, source_target_pairs={{0,16},{8,24},{16,0},{24,8},{1,17},{9,25},{17,1},{25,9},{2,18},{10... | collective-permute-start | bytes 835592 | tf_op jit(solution)/shard_map/ppermute | solution.py:845
  117.6 26.2 %collective-permute-start.30 = (bf16[128,1088]{1,0:T(8,128)(2,1)S(1)}, bf16[128,1088]{1,0:T(8,128)(2,1)}, u32[]{:S(2)}, u32[]{:S(2)}) collective-permute-start(bf16[128,1088]{1,0:T(8,128)(2,1)S(1)} %bitcast.180), channel_id=1, source_target_pairs={{0,8},{8,0},{16,24},{24,16},{1,9},{9,1},{17,25},{25,17},{2,10},{10... | collective-permute-start | bytes 835592 | tf_op jit(solution)/shard_map/ppermute | solution.py:845
  125.1 82.8 %collective-permute-start.43 = (bf16[128,272]{1,0:T(8,128)(2,1)}, bf16[128,272]{1,0:T(8,128)(2,1)}, u32[]{:S(2)}, u32[]{:S(2)}) collective-permute-start(bf16[128,272]{1,0:T(8,128)(2,1)} %get-tuple-element.226), channel_id=1, source_target_pairs={{0,8},{8,0},{16,24},{24,16},{1,9},{9,1},{17,25},{25,17},{2,10},{10... | collective-permute-start | bytes 208904 | tf_op jit(solution)/shard_map/ppermute | solution.py:845
  136.7 71.3 %collective-permute-start.44 = (bf16[128,272]{1,0:T(8,128)(2,1)}, bf16[128,272]{1,0:T(8,128)(2,1)}, u32[]{:S(2)}, u32[]{:S(2)}) collective-permute-start(bf16[128,272]{1,0:T(8,128)(2,1)} %get-tuple-element.225), channel_id=1, source_target_pairs={{0,16},{8,24},{16,0},{24,8},{1,17},{9,25},{17,1},{25,9},{2,18},{10... | collective-permute-start | bytes 208904 | tf_op jit(solution)/shard_map/ppermute | solution.py:845
  176.7 31.3 %collective-permute-start.45 = (bf16[128,272]{1,0:T(8,128)(2,1)S(1)}, bf16[128,272]{1,0:T(8,128)(2,1)}, u32[]{:S(2)}, u32[]{:S(2)}) collective-permute-start(bf16[128,272]{1,0:T(8,128)(2,1)S(1)} %copy-done.48), channel_id=1, source_target_pairs={{0,24},{8,16},{16,8},{24,0},{1,25},{9,17},{17,9},{25,1},{2,26},{10... | collective-permute-start | bytes 208904 | tf_op jit(solution)/shard_map/ppermute | solution.py:845
  183.0 30.5 %collective-permute-start.67 = (bf16[4,136,1088]{2,1,0:T(8,128)(2,1)}, bf16[4,136,1088]{2,1,0:T(8,128)(2,1)}, u32[]{:S(2)}, u32[]{:S(2)}) collective-permute-start(bf16[4,136,1088]{2,1,0:T(8,128)(2,1)} %constant_dynamic-slice_fusion.2), channel_id=1, source_target_pairs={{0,1},{1,0},{2,3},{3,2},{4,5},{5,4},{6,7},{7,6},{8,9},{9,8},{10,11... | collective-permute-start | bytes 3551240 | tf_op jit(solution)/shard_map/ppermute | solution.py:848
  189.3 31.1 %collective-permute-start.80 = (bf16[4,136,1088]{2,1,0:T(8,128)(2,1)}, bf16[4,136,1088]{2,1,0:T(8,128)(2,1)}, u32[]{:S(2)}, u32[]{:S(2)}) collective-permute-start(bf16[4,136,1088]{2,1,0:T(8,128)(2,1)} %dynamic-slice_bitcast_fusion), channel_id=1, source_target_pairs={{0,1},{1,0},{2,3},{3,2},{4,5},{5,4},{6,7},{7,6},{8,9},{9,8},{10,11... | collective-permute-start | bytes 3551240 | tf_op jit(solution)/shard_map/ppermute | solution.py:848
  230.6 32.4 %collective-permute-start.40 = (bf16[128,1088]{1,0:T(8,128)(2,1)}, bf16[128,1088]{1,0:T(8,128)(2,1)}, u32[]{:S(2)}, u32[]{:S(2)}) collective-permute-start(bf16[128,1088]{1,0:T(8,128)(2,1)} %get-tuple-element.215), channel_id=1, source_target_pairs={{0,8},{8,0},{16,24},{24,16},{1,9},{9,1},{17,25},{25,17},{2,10},{10... | collective-permute-start | bytes 835592 | tf_op jit(solution)/shard_map/ppermute | solution.py:845
  230.6 32.3 %collective-permute-start.41 = (bf16[128,1088]{1,0:T(8,128)(2,1)}, bf16[128,1088]{1,0:T(8,128)(2,1)}, u32[]{:S(2)}, u32[]{:S(2)}) collective-permute-start(bf16[128,1088]{1,0:T(8,128)(2,1)} %get-tuple-element.214), channel_id=1, source_target_pairs={{0,16},{8,24},{16,0},{24,8},{1,17},{9,25},{17,1},{25,9},{2,18},{10... | collective-permute-start | bytes 835592 | tf_op jit(solution)/shard_map/ppermute | solution.py:845
  234.0 28.9 %collective-permute-start.42 = (bf16[128,1088]{1,0:T(8,128)(2,1)}, bf16[128,1088]{1,0:T(8,128)(2,1)}, u32[]{:S(2)}, u32[]{:S(2)}) collective-permute-start(bf16[128,1088]{1,0:T(8,128)(2,1)} %get-tuple-element.213), channel_id=1, source_target_pairs={{0,24},{8,16},{16,8},{24,0},{1,25},{9,17},{17,9},{25,1},{2,26},{10... | collective-permute-start | bytes 835592 | tf_op jit(solution)/shard_map/ppermute | solution.py:845
  234.0 24.9 %collective-permute-start.48 = (bf16[136,960]{1,0:T(8,128)(2,1)}, bf16[136,960]{1,0:T(8,128)(2,1)}, u32[]{:S(2)}, u32[]{:S(2)}) collective-permute-start(bf16[136,960]{1,0:T(8,128)(2,1)} %get-tuple-element.220), channel_id=1, source_target_pairs={{0,16},{8,24},{16,0},{24,8},{1,17},{9,25},{17,1},{25,9},{2,18},{10... | collective-permute-start | bytes 783368 | tf_op jit(solution)/shard_map/ppermute | solution.py:845
  239.4 19.6 %collective-permute-start.49 = (bf16[136,960]{1,0:T(8,128)(2,1)}, bf16[136,960]{1,0:T(8,128)(2,1)}, u32[]{:S(2)}, u32[]{:S(2)}) collective-permute-start(bf16[136,960]{1,0:T(8,128)(2,1)} %get-tuple-element.219), channel_id=1, source_target_pairs={{0,24},{8,16},{16,8},{24,0},{1,25},{9,17},{17,9},{25,1},{2,26},{10... | collective-permute-start | bytes 783368 | tf_op jit(solution)/shard_map/ppermute | solution.py:845
  259.1 37.3 %collective-permute-start.71 = (bf16[2,136,1088]{2,1,0:T(8,128)(2,1)S(1)}, bf16[2,136,1088]{2,1,0:T(8,128)(2,1)}, u32[]{:S(2)}, u32[]{:S(2)}) collective-permute-start(bf16[2,136,1088]{2,1,0:T(8,128)(2,1)S(1)} %constant_dynamic-slice_fusion.1), channel_id=1, source_target_pairs={{0,2},{1,3},{2,0},{3,1},{4,6},{5,7},{6,4},{7,5},{8,10},{9,11},{10,... | collective-permute-start | bytes 1775624 | tf_op jit(solution)/shard_map/ppermute | solution.py:848
  279.3 21.0 %collective-permute-start.82 = (bf16[136,1088]{1,0:T(8,128)(2,1)S(1)}, bf16[136,1088]{1,0:T(8,128)(2,1)S(1)}, u32[]{:S(2)}, u32[]{:S(2)}) collective-permute-start(bf16[136,1088]{1,0:T(8,128)(2,1)S(1)} %dynamic-slice_bitcast_fusion.1), channel_id=1, source_target_pairs={{0,4},{1,5},{2,6},{3,7},{4,0},{5,1},{6,2},{7,3},{8,12},{9,13},{10,... | collective-permute-start | bytes 887816 | tf_op jit(solution)/shard_map/ppermute | solution.py:848
  280.3 27.3 %collective-permute-start.58 = (bf16[2,136,1088]{2,1,0:T(8,128)(2,1)S(1)}, bf16[2,136,1088]{2,1,0:T(8,128)(2,1)S(1)}, u32[]{:S(2)}, u32[]{:S(2)}) collective-permute-start(bf16[2,136,1088]{2,1,0:T(8,128)(2,1)S(1)} %constant_dynamic-slice_fusion.3), channel_id=1, source_target_pairs={{0,2},{1,3},{2,0},{3,1},{4,6},{5,7},{6,4},{7,5},{8,10},{9,11},{10,... | collective-permute-start | bytes 1775624 | tf_op jit(solution)/shard_map/ppermute | solution.py:848
  296.2 41.6 %collective-permute-start.57 = (bf16[128,1088]{1,0:T(8,128)(2,1)S(1)}, bf16[128,1088]{1,0:T(8,128)(2,1)S(1)}, u32[]{:S(2)}, u32[]{:S(2)}) collective-permute-start(bf16[128,1088]{1,0:T(8,128)(2,1)S(1)} %get-tuple-element.211), channel_id=1, source_target_pairs={{0,24},{8,16},{16,8},{24,0},{1,25},{9,17},{17,9},{25,1},{2,26},{10... | collective-permute-start | bytes 835592 | tf_op jit(solution)/shard_map/ppermute | solution.py:845
  296.3 41.7 %collective-permute-start.56 = (bf16[128,1088]{1,0:T(8,128)(2,1)S(1)}, bf16[128,1088]{1,0:T(8,128)(2,1)S(1)}, u32[]{:S(2)}, u32[]{:S(2)}) collective-permute-start(bf16[128,1088]{1,0:T(8,128)(2,1)S(1)} %get-tuple-element.212), channel_id=1, source_target_pairs={{0,16},{8,24},{16,0},{24,8},{1,17},{9,25},{17,1},{25,9},{2,18},{10... | collective-permute-start | bytes 835592 | tf_op jit(solution)/shard_map/ppermute | solution.py:845
  296.4 42.4 %collective-permute-start.55 = (bf16[128,1088]{1,0:T(8,128)(2,1)S(1)}, bf16[128,1088]{1,0:T(8,128)(2,1)S(1)}, u32[]{:S(2)}, u32[]{:S(2)}) collective-permute-start(bf16[128,1088]{1,0:T(8,128)(2,1)S(1)} %get-tuple-element.210), channel_id=1, source_target_pairs={{0,8},{8,0},{16,24},{24,16},{1,9},{9,1},{17,25},{25,17},{2,10},{10... | collective-permute-start | bytes 835592 | tf_op jit(solution)/shard_map/ppermute | solution.py:845
  307.6 30.1 %collective-permute-start.72 = (bf16[136,1088]{1,0:T(8,128)(2,1)S(1)}, bf16[136,1088]{1,0:T(8,128)(2,1)S(1)}, u32[]{:S(2)}, u32[]{:S(2)}) collective-permute-start(bf16[136,1088]{1,0:T(8,128)(2,1)S(1)} %dynamic-slice_bitcast_fusion.2), channel_id=1, source_target_pairs={{0,4},{1,5},{2,6},{3,7},{4,0},{5,1},{6,2},{7,3},{8,12},{9,13},{10,... | collective-permute-start | bytes 887816 | tf_op jit(solution)/shard_map/ppermute | solution.py:848
  307.9 36.7 %collective-permute-start.83 = (bf16[136,1088]{1,0:T(8,128)(2,1)S(1)}, bf16[136,1088]{1,0:T(8,128)(2,1)S(1)}, u32[]{:S(2)}, u32[]{:S(2)}) collective-permute-start(bf16[136,1088]{1,0:T(8,128)(2,1)S(1)} %fusion.16.refs_0_), channel_id=1, source_target_pairs={{0,4},{1,5},{2,6},{3,7},{4,0},{5,1},{6,2},{7,3},{8,12},{9,13},{10,... | collective-permute-start | bytes 887816 | tf_op jit(solution)/shard_map/ppermute | solution.py:848
  337.8 20.2 %collective-permute-start.59 = (bf16[136,1088]{1,0:T(8,128)(2,1)S(1)}, bf16[136,1088]{1,0:T(8,128)(2,1)S(1)}, u32[]{:S(2)}, u32[]{:S(2)}) collective-permute-start(bf16[136,1088]{1,0:T(8,128)(2,1)S(1)} %dynamic-slice_bitcast_fusion.7), channel_id=1, source_target_pairs={{0,4},{1,5},{2,6},{3,7},{4,0},{5,1},{6,2},{7,3},{8,12},{9,13},{10,... | collective-permute-start | bytes 887816 | tf_op jit(solution)/shard_map/ppermute | solution.py:848
  337.9 21.7 %collective-permute-start.84 = (bf16[136,1088]{1,0:T(8,128)(2,1)S(1)}, bf16[136,1088]{1,0:T(8,128)(2,1)S(1)}, u32[]{:S(2)}, u32[]{:S(2)}) collective-permute-start(bf16[136,1088]{1,0:T(8,128)(2,1)S(1)} %fusion.16.refs_0_), channel_id=1, source_target_pairs={{0,2},{1,3},{2,0},{3,1},{4,6},{5,7},{6,4},{7,5},{8,10},{9,11},{10,... | collective-permute-start | bytes 887816 | tf_op jit(solution)/shard_map/ppermute | solution.py:848
  338.0 21.7 %collective-permute-start.86 = (bf16[136,1088]{1,0:T(8,128)(2,1)S(1)}, bf16[136,1088]{1,0:T(8,128)(2,1)S(1)}, u32[]{:S(2)}, u32[]{:S(2)}) collective-permute-start(bf16[136,1088]{1,0:T(8,128)(2,1)S(1)} %fusion.16.refs_0_), channel_id=1, source_target_pairs={{0,1},{1,0},{2,3},{3,2},{4,5},{5,4},{6,7},{7,6},{8,9},{9,8},{10,11... | collective-permute-start | bytes 887816 | tf_op jit(solution)/shard_map/ppermute | solution.py:848
  338.8 26.0 %collective-permute-start.73 = (bf16[136,1088]{1,0:T(8,128)(2,1)S(1)}, bf16[136,1088]{1,0:T(8,128)(2,1)}, u32[]{:S(2)}, u32[]{:S(2)}) collective-permute-start(bf16[136,1088]{1,0:T(8,128)(2,1)S(1)} %fusion.17.refs_0_), channel_id=1, source_target_pairs={{0,4},{1,5},{2,6},{3,7},{4,0},{5,1},{6,2},{7,3},{8,12},{9,13},{10,... | collective-permute-start | bytes 887816 | tf_op jit(solution)/shard_map/ppermute | solution.py:848
  344.5 27.0 %collective-permute-start.74 = (bf16[136,1088]{1,0:T(8,128)(2,1)S(1)}, bf16[136,1088]{1,0:T(8,128)(2,1)}, u32[]{:S(2)}, u32[]{:S(2)}) collective-permute-start(bf16[136,1088]{1,0:T(8,128)(2,1)S(1)} %fusion.17.refs_0_), channel_id=1, source_target_pairs={{0,2},{1,3},{2,0},{3,1},{4,6},{5,7},{6,4},{7,5},{8,10},{9,11},{10,... | collective-permute-start | bytes 887816 | tf_op jit(solution)/shard_map/ppermute | solution.py:848
  359.6 19.8 %collective-permute-start.85 = (bf16[136,1088]{1,0:T(8,128)(2,1)S(1)}, bf16[136,1088]{1,0:T(8,128)(2,1)}, u32[]{:S(2)}, u32[]{:S(2)}) collective-permute-start(bf16[136,1088]{1,0:T(8,128)(2,1)S(1)} %collective-permute-done.83.refs_1_), channel_id=1, source_target_pairs={{0,2},{1,3},{2,0},{3,1},{4,6},{5,7},{6,4},{7,5},{8,10},{9,11},{10,... | collective-permute-start | bytes 887816 | tf_op jit(solution)/shard_map/ppermute | solution.py:848
  359.7 20.3 %collective-permute-start.87 = (bf16[136,1088]{1,0:T(8,128)(2,1)S(1)}, bf16[136,1088]{1,0:T(8,128)(2,1)S(1)}, u32[]{:S(2)}, u32[]{:S(2)}) collective-permute-start(bf16[136,1088]{1,0:T(8,128)(2,1)S(1)} %collective-permute-done.83.refs_1_), channel_id=1, source_target_pairs={{0,1},{1,0},{2,3},{3,2},{4,5},{5,4},{6,7},{7,6},{8,9},{9,8},{10,11... | collective-permute-start | bytes 887816 | tf_op jit(solution)/shard_map/ppermute | solution.py:848
  371.5 20.0 %collective-permute-start.75 = (bf16[136,1088]{1,0:T(8,128)(2,1)}, bf16[136,1088]{1,0:T(8,128)(2,1)S(1)}, u32[]{:S(2)}, u32[]{:S(2)}) collective-permute-start(bf16[136,1088]{1,0:T(8,128)(2,1)} %collective-permute-done.73.refs_1_), channel_id=1, source_target_pairs={{0,2},{1,3},{2,0},{3,1},{4,6},{5,7},{6,4},{7,5},{8,10},{9,11},{10,... | collective-permute-start | bytes 887816 | tf_op jit(solution)/shard_map/ppermute | solution.py:848
  371.5 20.0 %collective-permute-start.60 = (bf16[136,1088]{1,0:T(8,128)(2,1)}, bf16[136,1088]{1,0:T(8,128)(2,1)}, u32[]{:S(2)}, u32[]{:S(2)}) collective-permute-start(bf16[136,1088]{1,0:T(8,128)(2,1)} %fusion.18.refs_0_), channel_id=1, source_target_pairs={{0,4},{1,5},{2,6},{3,7},{4,0},{5,1},{6,2},{7,3},{8,12},{9,13},{10,... | collective-permute-start | bytes 887816 | tf_op jit(solution)/shard_map/ppermute | solution.py:848
  380.0 16.9 %collective-permute-start.78 = (bf16[136,1088]{1,0:T(8,128)(2,1)}, bf16[136,1088]{1,0:T(8,128)(2,1)}, u32[]{:S(2)}, u32[]{:S(2)}) collective-permute-start(bf16[136,1088]{1,0:T(8,128)(2,1)} %collective-permute-done.74.refs_2_), channel_id=1, source_target_pairs={{0,1},{1,0},{2,3},{3,2},{4,5},{5,4},{6,7},{7,6},{8,9},{9,8},{10,11... | collective-permute-start | bytes 887816 | tf_op jit(solution)/shard_map/ppermute | solution.py:848
  380.1 16.9 %collective-permute-start.89 = (bf16[136,1088]{1,0:T(8,128)(2,1)}, bf16[136,1088]{1,0:T(8,128)(2,1)}, u32[]{:S(2)}, u32[]{:S(2)}) collective-permute-start(bf16[136,1088]{1,0:T(8,128)(2,1)} %collective-permute-done.85.refs_3_), channel_id=1, source_target_pairs={{0,1},{1,0},{2,3},{3,2},{4,5},{5,4},{6,7},{7,6},{8,9},{9,8},{10,11... | collective-permute-start | bytes 887816 | tf_op jit(solution)/shard_map/ppermute | solution.py:848
  395.8 24.7 %collective-permute-start.63 = (bf16[136,1088]{1,0:T(8,128)(2,1)}, bf16[136,1088]{1,0:T(8,128)(2,1)S(1)}, u32[]{:S(2)}, u32[]{:S(2)}) collective-permute-start(bf16[136,1088]{1,0:T(8,128)(2,1)} %fusion.18.refs_0_), channel_id=1, source_target_pairs={{0,1},{1,0},{2,3},{3,2},{4,5},{5,4},{6,7},{7,6},{8,9},{9,8},{10,11... | collective-permute-start | bytes 887816 | tf_op jit(solution)/shard_map/ppermute | solution.py:848
  396.9 18.3 %collective-permute-start.79 = (bf16[136,1088]{1,0:T(8,128)(2,1)}, bf16[136,1088]{1,0:T(8,128)(2,1)S(1)}, u32[]{:S(2)}, u32[]{:S(2)}) collective-permute-start(bf16[136,1088]{1,0:T(8,128)(2,1)} %copy-done.20), channel_id=1, source_target_pairs={{0,1},{1,0},{2,3},{3,2},{4,5},{5,4},{6,7},{7,6},{8,9},{9,8},{10,11... | collective-permute-start | bytes 887816 | tf_op jit(solution)/shard_map/ppermute | solution.py:848
  397.0 23.6 %collective-permute-start.64 = (bf16[136,1088]{1,0:T(8,128)(2,1)}, bf16[136,1088]{1,0:T(8,128)(2,1)}, u32[]{:S(2)}, u32[]{:S(2)}) collective-permute-start(bf16[136,1088]{1,0:T(8,128)(2,1)} %collective-permute-done.60.refs_1_), channel_id=1, source_target_pairs={{0,1},{1,0},{2,3},{3,2},{4,5},{5,4},{6,7},{7,6},{8,9},{9,8},{10,11... | collective-permute-start | bytes 887816 | tf_op jit(solution)/shard_map/ppermute | solution.py:848
  400.4 20.2 %collective-permute-start.65 = (bf16[136,1088]{1,0:T(8,128)(2,1)}, bf16[136,1088]{1,0:T(8,128)(2,1)}, u32[]{:S(2)}, u32[]{:S(2)}) collective-permute-start(bf16[136,1088]{1,0:T(8,128)(2,1)} %collective-permute-done.61.refs_2_), channel_id=1, source_target_pairs={{0,1},{1,0},{2,3},{3,2},{4,5},{5,4},{6,7},{7,6},{8,9},{9,8},{10,11... | collective-permute-start | bytes 887816 | tf_op jit(solution)/shard_map/ppermute | solution.py:848
  (110 other events, 2107.4 us)
